TPU v7x, 32 devices: a whole 2x2x4 slice. The times are simulated.
32 devices in a mesh: clip: 2 (over core), tm: 16 (over z, y, x).
Axes of the slice: x: 2, y: 2, z: 4, core: 2. Of those that a mesh axis runs over, the one named last changes fastest.
Arguments:
- clip_frames: bfloat16 [2, 32, 64, 64, 128], P('clip', 'tm'), may hold values from -6 to 6
- spatial_weight: bfloat16 [3, 3, 128, 256], replicated, may hold values from -0.1875 to 0.1875
- norm_gain: float32 [256], replicated, may hold values from 0.5 to 1.5
- norm_bias: float32 [256], replicated, may hold values from -3 to 3
- temporal_weight: bfloat16 [3, 256, 256], replicated, may hold values from -0.21875 to 0.21875
- cotangent: bfloat16 [2, 32, 32, 32, 256], P('clip', 'tm'), may hold values from -0.0234375 to 0.0234375
Outputs:
- mixed: bfloat16 [2, 32, 32, 32, 256], P('clip', 'tm')
- spatial_grad: float32 [3, 3, 128, 256], replicated
- gain_grad: float32 [256], replicated
- bias_grad: float32 [256], replicated
- temporal_grad: float32 [3, 256, 256], replicated
All inputs are finite; a program needn't handle non-finite values.
Results may differ from a plain program's by a relative error of at most 0.0085.
Values may be sent and summed in bfloat16 or wider, within the bound.
A program may use at most 64 MiB of HBM per device.

v0:
```python
import jax
import jax.numpy as jnp
from jax import lax
from jax.sharding import PartitionSpec as P

GROUPS = 32
DILATION_FRAMES = 4


epsilon = 1e-05


def delay_rows(values):
    return jnp.pad(values, ((0, 0), (1, 0), (0, 0), (0, 0)))[:, :-1]


def delay_cols(values):
    return jnp.pad(values, ((0, 0), (0, 0), (1, 0), (0, 0)))[:, :, :-1]


def advance_rows(values):
    return jnp.pad(values, ((0, 0), (0, 1), (0, 0), (0, 0)))[:, 1:]


def advance_cols(values):
    return jnp.pad(values, ((0, 0), (0, 0), (0, 1), (0, 0)))[:, :, 1:]


def split_phases(frames_in):
    frames, height, width, chans = frames_in.shape
    viewed = frames_in.reshape(frames, height // 2, 2, width // 2, 2, chans)
    phases = {}
    for row_phase in range(2):
        for col_phase in range(2):
            phases[row_phase, col_phase] = viewed[:, :, row_phase, :, col_phase, :].reshape(
                -1, chans
            )
    return phases


def tap_layout(offset):
    return (0 if offset == 1 else 1, offset == 0)


def membership(chans):
    channel_group = lax.broadcasted_iota(jnp.int32, (chans, GROUPS), 0) // (chans // GROUPS)
    group_index = lax.broadcasted_iota(jnp.int32, (chans, GROUPS), 1)
    return (channel_group == group_index).astype(jnp.float32)


def activate(conv_out, gain, bias):
    chans = conv_out.shape[-1]
    member = membership(chans)
    count = conv_out.shape[1] * conv_out.shape[2] * (chans // GROUPS)
    high = lax.Precision.HIGHEST
    chan_sum = jnp.sum(conv_out, axis=(1, 2))
    group_mean = jnp.dot(chan_sum, member, precision=high) / count
    center = jnp.dot(group_mean, member.T, precision=high)
    deviation = conv_out - center[:, None, None, :]
    chan_square = jnp.sum(deviation * deviation, axis=(1, 2))
    group_var = jnp.dot(chan_square, member, precision=high) / count
    scaling = jnp.dot(lax.rsqrt(group_var + epsilon), member.T, precision=high)
    normed = deviation * scaling[:, None, None, :]
    return jax.nn.silu(normed * gain + bias)


def padded_lag(values, frame_offset):
    if frame_offset == 0:
        return values
    frames = values.shape[0]
    if frame_offset > 0:
        filler = jnp.zeros((frame_offset,) + values.shape[1:], values.dtype)
        return jnp.concatenate([filler, values[: frames - frame_offset]], axis=0)
    filler = jnp.zeros((-frame_offset,) + values.shape[1:], values.dtype)
    return jnp.concatenate([values[-frame_offset:], filler], axis=0)


def temporal_pass(acts, grads, weight, lag_rule):
    chans = acts.shape[-1]
    total = acts.astype(jnp.float32)
    backward_total_sum = grads.astype(jnp.float32)
    tap_grads = []
    flattened_gradients = grads.reshape(-1, chans)
    for kernel_tap_index in range(3):
        frame_offset = kernel_tap_index * DILATION_FRAMES
        earlier = lag_rule(acts, frame_offset).reshape(-1, chans)
        later = lag_rule(grads, -frame_offset).reshape(-1, chans)
        total = total + jnp.dot(
            earlier, weight[kernel_tap_index], preferred_element_type=jnp.float32
        ).reshape(acts.shape)
        backward_total_sum = backward_total_sum + jnp.dot(
            later, weight[kernel_tap_index].T, preferred_element_type=jnp.float32
        ).reshape(acts.shape)
        tap_grads.append(
            lax.dot_general(
                earlier,
                flattened_gradients,
                (((0,), (0,)), ((), ())),
                preferred_element_type=jnp.float32,
            )
        )
    return (
        total.astype(jnp.bfloat16),
        backward_total_sum.astype(jnp.bfloat16),
        jnp.stack(tap_grads),
    )


def per_device(clip_frames, spatial_weight, norm_gain, norm_bias, temporal_weight, cotangent):
    frames_in = clip_frames[0]
    upstream = cotangent[0]
    frames, height, width, _ = frames_in.shape
    out_chans = spatial_weight.shape[-1]
    out_shape = (frames, height // 2, width // 2, out_chans)
    phases = split_phases(frames_in)
    partial_sums = {}
    for row_offset in range(3):
        row_phase, row_delay = tap_layout(row_offset)
        for col_offset in range(3):
            col_phase, col_delay = tap_layout(col_offset)
            product = jnp.dot(
                phases[row_phase, col_phase],
                spatial_weight[row_offset, col_offset],
                preferred_element_type=jnp.float32,
            )
            key_pair = (row_delay, col_delay)
            if key_pair in partial_sums:
                partial_sums[key_pair] = partial_sums[key_pair] + product
            else:
                partial_sums[key_pair] = product
    conv_out = partial_sums[False, False].reshape(out_shape)
    conv_out = conv_out + delay_rows(partial_sums[True, False].reshape(out_shape))
    conv_out = conv_out + delay_cols(partial_sums[False, True].reshape(out_shape))
    conv_out = conv_out + delay_rows(delay_cols(partial_sums[True, True].reshape(out_shape)))
    activated, pullback = jax.vjp(activate, conv_out, norm_gain, norm_bias)
    acts = activated.astype(jnp.bfloat16)
    act_rows = lax.all_to_all(acts, "tm", split_axis=1, concat_axis=0, tiled=True)
    grad_rows = lax.all_to_all(upstream, "tm", split_axis=1, concat_axis=0, tiled=True)
    mixed_rows, act_grad_rows, temporal_part = temporal_pass(
        act_rows, grad_rows, temporal_weight, padded_lag
    )
    mixed = lax.all_to_all(mixed_rows, "tm", split_axis=0, concat_axis=1, tiled=True)
    act_grad = lax.all_to_all(act_grad_rows, "tm", split_axis=0, concat_axis=1, tiled=True)
    conv_grad, gain_partial_sum, bias_part = pullback(act_grad.astype(jnp.float32))
    conv_grad = conv_grad.astype(jnp.bfloat16)
    grad_versions = {
        (False, False): conv_grad.reshape(-1, out_chans),
        (True, False): advance_rows(conv_grad).reshape(-1, out_chans),
        (False, True): advance_cols(conv_grad).reshape(-1, out_chans),
        (True, True): advance_rows(advance_cols(conv_grad)).reshape(-1, out_chans),
    }
    tap_rows = []
    for row_offset in range(3):
        row_phase, row_delay = tap_layout(row_offset)
        tap_row = []
        for col_offset in range(3):
            col_phase, col_delay = tap_layout(col_offset)
            tap_row.append(
                lax.dot_general(
                    phases[row_phase, col_phase],
                    grad_versions[row_delay, col_delay],
                    (((0,), (0,)), ((), ())),
                    preferred_element_type=jnp.float32,
                )
            )
        tap_rows.append(jnp.stack(tap_row))
    spatial_part = jnp.stack(tap_rows)
    spatial_gradient_total, gain_total, bias_total, temporal_total = lax.psum(
        (spatial_part, gain_partial_sum, bias_part, temporal_part), ("clip", "tm")
    )
    return (mixed[None], spatial_gradient_total, gain_total, bias_total, temporal_total)


def solution(mesh):
    return jax.shard_map(
        per_device,
        mesh=mesh,
        in_specs=(
            P("clip", "tm", None, None, None),
            P(),
            P(),
            P(),
            P(),
            P("clip", "tm", None, None, None),
        ),
        out_specs=(P("clip", "tm", None, None, None), P(), P(), P(), P()),
        check_vma=False,
    )
```

profile of v0, /device:TPU:0, one launch (start us, length us, event | category | flops | bytes accessed | tf_op | source)
XLA Modules:
  0.0 279.1 jit_solution(15549774472298984337)
XLA Ops:
  7.2 2.4 copy.71
  9.6 8.4 %all-to-all-start.2 = ((bf16[2,32,32,256]{3,2,0,1:T(8,128)(2,1)}), bf16[2,32,32,256]{3,2,0,1:T(8,128)(2,1)}, u32[]{:S(2)}, u32[]{:S(2)}) async-start(bf16[2,32,32,256]{3,2,0,1:T(8,128)(2,1)} %bitcast.205), calls=%async_computation.2 | async-start | bytes 2097152 | tf_op jit(solution)/shard_map/all_to_all | solution.py:138
  18.0 4.5 %fusion.86 = (bf16[2,32,1,32,1,128]{5,4,3,2,1,0:T(2,128)(2,1)S(1)}, bf16[2,32,1,32,1,128]{5,4,3,2,1,0:T(2,128)(2,1)S(1)}, bf16[2,32,1,32,1,128]{5,4,3,2,1,0:T(2,128)(2,1)S(1)}, bf16[2,32,1,32,1,128]{5,4,3,2,1,0:T(2,128)(2,1)S(1)}) fusion(bf16[2,32,2,32,2,128]{5,4,3,2,1,0:T(2,128)(2,1)S(1)} %bitcast.240), kind=kLoop, calls=%fused_computation.138 | loop fusion | bytes 4194304 | tf_op jit(solution)/shard_map/slice | solution.py:35
  24.1 1.8 fusion.32
  25.9 1.8 fusion.7
  28.1 1.8 convolution_add_fusion.3
  29.9 1.7 convolution_add_fusion.1
  31.6 10.9 %all-to-all-done.2 = bf16[2,32,32,256]{3,2,0,1:T(8,128)(2,1)} async-done(((bf16[2,32,32,256]{3,2,0,1:T(8,128)(2,1)}), bf16[2,32,32,256]{3,2,0,1:T(8,128)(2,1)}, u32[]{:S(2)}, u32[]{:S(2)}) %all-to-all-start.2) | async-done | bytes 1048608 | tf_op jit(solution)/shard_map/all_to_all | solution.py:138
  42.5 1.3 copy.72
  43.9 0.9 copy-done.13
  45.7 1.6 add_convert_fusion.1
  47.3 5.9 %all-to-all-start.3 = ((bf16[32,2,32,256]{3,2,1,0:T(8,128)(2,1)}), bf16[32,2,32,256]{3,2,1,0:T(8,128)(2,1)}, u32[]{:S(2)}, u32[]{:S(2)}) async-start(bf16[32,2,32,256]{3,2,1,0:T(8,128)(2,1)} %add_convert_fusion.1), calls=%async_computation.3 | async-start | bytes 2097152 | tf_op jit(solution)/shard_map/all_to_all | solution.py:143
  53.2 2.1 pad_slice_fusion
  55.4 1.4 convolution_add_fusion
  57.1 0.6 copy-done.10
  57.7 1.8 fusion.84
  61.1 0.6 copy-done.32
  62.0 14.2 %all-to-all-done.3 = bf16[32,2,32,256]{3,2,1,0:T(8,128)(2,1)} async-done(((bf16[32,2,32,256]{3,2,1,0:T(8,128)(2,1)}), bf16[32,2,32,256]{3,2,1,0:T(8,128)(2,1)}, u32[]{:S(2)}, u32[]{:S(2)}) %all-to-all-start.3) | async-done | bytes 1048608 | tf_op jit(solution)/shard_map/all_to_all | solution.py:143
  76.2 1.5 copy.43
  77.8 3.2 %fusion.82 = (f32[256]{0:T(256)}, f32[2,256]{1,0:T(2,128)S(1)}, f32[2,32,32,256]{3,2,1,0:T(8,128)}, bf16[2,32,32,256]{3,2,1,0:T(8,128)(2,1)S(1)}) fusion(f32[256]{0:T(256)S(1)} %copy-done.17, f32[2,32,32,256]{3,2,1,0:T(8,128)S(1)} %get-tuple-element.40, f32[2,256]{1,0:T(2,128)S(1)} %fusion.23, f32[2,32,32,256]{3,2,1,0:T(8,128)S(1)} %bitcast.239, ...), kind=kLoop, calls=%fused_computation.136 | loop fusion | flops 9960704 | bytes 7349248 | tf_op jit(solution)/shard_map/transpose(jvp())/reduce_sum | solution.py:64
  81.6 1.1 copy.36
  82.7 6.1 %all-to-all-start = ((bf16[2,32,32,256]{3,2,0,1:T(8,128)(2,1)}), bf16[2,32,32,256]{3,2,0,1:T(8,128)(2,1)}, u32[]{:S(2)}, u32[]{:S(2)}) async-start(bf16[2,32,32,256]{3,2,0,1:T(8,128)(2,1)} %copy.36), calls=%async_computation | async-start | bytes 2097152 | tf_op jit(solution)/shard_map/all_to_all | solution.py:137
  88.8 2.9 %multiply_reduce_fusion = (f32[256]{0:T(256)}, f32[2,256]{1,0:T(2,128)S(1)}) fusion(f32[2,32,32,256]{3,2,1,0:T(8,128)} %get-tuple-element.38, f32[2,32,32,256]{3,2,1,0:T(8,128)S(1)} %get-tuple-element.40, f32[2,256]{1,0:T(2,128)S(1)} %fusion.22, f32[2,256]{1,0:T(2,128)S(1)} %fusion.23, f32[2,256]{1,0:T(2,128)S(1)} %fusion.21, f32[256]{0:T(256)S(1)} %copy-done.17), kind=kLoop, calls=%fused_computation.16 | loop fusion | flops 5242112 | bytes 4204544 | tf_op jit(solution)/shard_map/transpose(jvp())/reduce_sum | solution.py:64
  92.4 0.7 add_convert_fusion
  93.0 0.7 pad_slice_fusion.5
  94.8 0.5 convolution_bitcast_fusion.9
  95.3 0.5 convolution_bitcast_fusion.11
  95.9 0.5 convolution_bitcast_fusion.7
  96.4 0.5 convolution_bitcast_fusion.6
  96.9 0.5 convolution_bitcast_fusion.8
  97.4 0.8 maximum_bitcast_fusion.1
  98.1 0.5 convolution_bitcast_fusion.5
  98.6 0.5 convolution_bitcast_fusion.4
  99.1 0.5 convolution_bitcast_fusion.3
  99.6 0.8 maximum_bitcast_fusion.2
  100.4 11.3 %all-to-all-done = bf16[2,32,32,256]{3,2,0,1:T(8,128)(2,1)} async-done(((bf16[2,32,32,256]{3,2,0,1:T(8,128)(2,1)}), bf16[2,32,32,256]{3,2,0,1:T(8,128)(2,1)}, u32[]{:S(2)}, u32[]{:S(2)}) %all-to-all-start) | async-done | bytes 1048608 | tf_op jit(solution)/shard_map/all_to_all | solution.py:137
  111.7 1.3 copy.73
  114.0 1.5 add_convert_fusion.2
  115.5 6.2 %all-to-all-start.1 = ((bf16[32,2,32,256]{3,2,1,0:T(8,128)(2,1)}), bf16[32,2,32,256]{3,2,1,0:T(8,128)(2,1)}, u32[]{:S(2)}, u32[]{:S(2)}) async-start(bf16[32,2,32,256]{3,2,1,0:T(8,128)(2,1)} %add_convert_fusion.2), calls=%async_computation.1 | async-start | bytes 2097152 | tf_op jit(solution)/shard_map/all_to_all | solution.py:142
  121.7 2.1 pad_maximum_fusion
  124.1 0.5 convolution_bitcast_fusion.1
  125.0 2.0 convolution_bitcast_fusion.2
  127.1 0.9 pad_maximum_fusion.1
  128.1 43.7 %all-reduce.11 = (f32[256]{0:T(256)}, f32[256]{0:T(256)}) all-reduce(f32[256]{0:T(256)S(1)} %copy-done.19, f32[256]{0:T(256)S(1)} %copy-done.18), channel_id=1, replica_groups=mesh['clip'=2,'tm'=16] {'clip','tm'}, use_global_device_ids=true, to_apply=%region_6.7 | all-reduce | flops 512 | bytes 4096 | tf_op jit(solution)/shard_map/psum | solution.py:168
  171.7 94.6 %all-reduce.15.cloned.1.call-done = (f32[3,3,128,256]{2,3,1,0:T(8,128)}, f32[3,256,256]{2,1,0:T(8,128)}) async-done(((f32[3,3,128,256]{2,3,1,0:T(8,128)}, f32[3,256,256]{2,1,0:T(8,128)}), (f32[3,3,128,256]{2,3,1,0:T(8,128)}, f32[3,256,256]{2,1,0:T(8,128)})) %all-reduce.15.cloned.1.call-update) | async-done | bytes 1966096 | tf_op jit(solution)/shard_map/psum | solution.py:168
  266.4 2.7 copy.44
  269.1 2.3 copy.39
  271.4 0.9 copy.76
  (100 shorter events, 9.4 us)
Async XLA Ops:
  7.2 10.8 %copy-start.8 = (bf16[1,2,64,64,128]{4,3,2,1,0:T(8,128)(2,1)S(1)}, bf16[1,2,64,64,128]{4,3,2,1,0:T(8,128)(2,1)}, u32[]{:S(2)}) copy-start(bf16[1,2,64,64,128]{4,3,2,1,0:T(8,128)(2,1)} %param.6) | copy-start | bytes 6291460
  9.6 32.9 %all-to-all-start.2 = ((bf16[2,32,32,256]{3,2,0,1:T(8,128)(2,1)}), bf16[2,32,32,256]{3,2,0,1:T(8,128)(2,1)}, u32[]{:S(2)}, u32[]{:S(2)}) async-start(bf16[2,32,32,256]{3,2,0,1:T(8,128)(2,1)} %bitcast.205), calls=%async_computation.2 | async-start | bytes 2097152 | tf_op jit(solution)/shard_map/all_to_all | solution.py:138
  18.0 4.6 %copy-start.16 = (bf16[3,3,128,256]{3,2,1,0:T(8,128)(2,1)S(1)}, bf16[3,3,128,256]{3,2,1,0:T(8,128)(2,1)}, u32[]{:S(2)}) copy-start(bf16[3,3,128,256]{3,2,1,0:T(8,128)(2,1)} %param.7) | copy-start | bytes 1769476
  22.6 0.8 copy-start.11
  23.4 36.4 %copy-start.21 = (s32[256]{0:T(256)}, s32[256]{0:T(256)S(1)}, u32[]{:S(2)}) copy-start(s32[256]{0:T(256)S(1)} %get-tuple-element.52) | copy-start | bytes 3076
  23.4 36.4 %copy-start.25 = (s32[256]{0:T(256)}, s32[256]{0:T(256)S(1)}, u32[]{:S(2)}) copy-start(s32[256]{0:T(256)S(1)} %get-tuple-element.53) | copy-start | bytes 3076
  23.5 4.2 %copy-start.5 = (bf16[2,32,1,32,1,128]{5,3,4,2,1,0:T(8,128)(2,1)}, bf16[2,32,1,32,1,128]{5,3,4,2,1,0:T(8,128)(2,1)S(1)}, u32[]{:S(2)}) copy-start(bf16[2,32,1,32,1,128]{5,3,4,2,1,0:T(8,128)(2,1)S(1)} %copy.55) | copy-start | bytes 1572868
  23.6 4.6 %copy-start.3 = (bf16[2,32,1,32,1,128]{5,3,4,2,1,0:T(8,128)(2,1)}, bf16[2,32,1,32,1,128]{5,3,4,2,1,0:T(8,128)(2,1)S(1)}, u32[]{:S(2)}) copy-start(bf16[2,32,1,32,1,128]{5,3,4,2,1,0:T(8,128)(2,1)S(1)} %copy.56) | copy-start | bytes 1572868
  23.7 31.6 %copy-start = (bf16[2,32,1,32,1,128]{5,3,1,0,4,2:T(8,128)(2,1)}, bf16[2,32,1,32,1,128]{5,3,1,0,4,2:T(8,128)(2,1)S(1)}, u32[]{:S(2)}) copy-start(bf16[2,32,1,32,1,128]{5,3,1,0,4,2:T(8,128)(2,1)S(1)} %copy.57) | copy-start | bytes 1572868
  43.8 1.0 copy-start.13
  47.3 28.9 %all-to-all-start.3 = ((bf16[32,2,32,256]{3,2,1,0:T(8,128)(2,1)}), bf16[32,2,32,256]{3,2,1,0:T(8,128)(2,1)}, u32[]{:S(2)}, u32[]{:S(2)}) async-start(bf16[32,2,32,256]{3,2,1,0:T(8,128)(2,1)} %add_convert_fusion.1), calls=%async_computation.3 | async-start | bytes 2097152 | tf_op jit(solution)/shard_map/all_to_all | solution.py:143
  53.2 7.9 %copy-start.29 = (pred[256]{0:T(512)(128)(4,1)}, pred[256]{0:T(512)(128)(4,1)S(1)}, u32[]{:S(2)}) copy-start(pred[256]{0:T(512)(128)(4,1)S(1)} %compare_and_fusion) | copy-start | bytes 772
  53.2 2.2 copy-start.7
  55.4 1.6 copy-start.9
  55.4 2.3 copy-start.10
  60.0 0.7 copy-start.22
  60.0 0.8 copy-start.26
  60.8 16.9 %copy-start.17 = (f32[256]{0:T(256)S(1)}, f32[256]{0:T(256)}, u32[]{:S(2)}) copy-start(f32[256]{0:T(256)} %param.8) | copy-start | bytes 3076
  60.8 16.9 %copy-start.20 = (f32[256]{0:T(256)S(1)}, f32[256]{0:T(256)}, u32[]{:S(2)}) copy-start(f32[256]{0:T(256)} %param.9) | copy-start | bytes 3076
  61.1 0.6 copy-start.32
  77.7 3.3 %copy-start.23 = (s32[256]{0:T(256)S(1)}, s32[256]{0:T(256)}, u32[]{:S(2)}) copy-start(s32[256]{0:T(256)} %copy-done.21) | copy-start | bytes 3076
  77.7 3.3 %copy-start.27 = (s32[256]{0:T(256)S(1)}, s32[256]{0:T(256)}, u32[]{:S(2)}) copy-start(s32[256]{0:T(256)} %copy-done.25) | copy-start | bytes 3076
  77.7 3.3 %copy-start.30 = (pred[256]{0:T(512)(128)(4,1)S(1)}, pred[256]{0:T(512)(128)(4,1)}, u32[]{:S(2)}) copy-start(pred[256]{0:T(512)(128)(4,1)} %copy-done.29) | copy-start | bytes 772
  77.7 3.3 %copy-start.33 = (f32[2,32]{1,0:T(2,128)S(1)}, f32[2,32]{1,0:T(2,128)}, u32[]{:S(2)}) copy-start(f32[2,32]{1,0:T(2,128)} %copy-done.32) | copy-start | bytes 772
  82.7 28.9 %all-to-all-start = ((bf16[2,32,32,256]{3,2,0,1:T(8,128)(2,1)}), bf16[2,32,32,256]{3,2,0,1:T(8,128)(2,1)}, u32[]{:S(2)}, u32[]{:S(2)}) async-start(bf16[2,32,32,256]{3,2,0,1:T(8,128)(2,1)} %copy.36), calls=%async_computation | async-start | bytes 2097152 | tf_op jit(solution)/shard_map/all_to_all | solution.py:137
  88.8 3.0 %copy-start.24 = (s32[256]{0:T(256)S(1)}, s32[256]{0:T(256)}, u32[]{:S(2)}) copy-start(s32[256]{0:T(256)} %copy-done.21) | copy-start | bytes 3076
  88.8 3.0 %copy-start.28 = (s32[256]{0:T(256)S(1)}, s32[256]{0:T(256)}, u32[]{:S(2)}) copy-start(s32[256]{0:T(256)} %copy-done.25) | copy-start | bytes 3076
  88.8 3.0 %copy-start.31 = (pred[256]{0:T(512)(128)(4,1)S(1)}, pred[256]{0:T(512)(128)(4,1)}, u32[]{:S(2)}) copy-start(pred[256]{0:T(512)(128)(4,1)} %copy-done.29) | copy-start | bytes 772
  88.8 3.5 %copy-start.2 = (f32[2,32,32,256]{3,2,1,0:T(8,128)S(1)}, f32[2,32,32,256]{3,2,1,0:T(8,128)}, u32[]{:S(2)}) copy-start(f32[2,32,32,256]{3,2,1,0:T(8,128)} %get-tuple-element.38) | copy-start | bytes 6291460
  93.0 1.0 copy-start.4
  93.8 1.1 copy-start.1
  94.8 1.0 copy-start.12
  95.3 1.1 copy-start.6
  115.5 6.3 %copy-start.14 = (f32[1,3,128,256]{2,3,1,0:T(8,128)S(1)}, f32[1,3,128,256]{2,3,1,0:T(8,128)}, u32[]{:S(2)}) copy-start(f32[1,3,128,256]{2,3,1,0:T(8,128)} %maximum_bitcast_fusion.1) | copy-start | bytes 1179652
  115.5 153.6 %all-to-all-start.1 = ((bf16[32,2,32,256]{3,2,1,0:T(8,128)(2,1)}), bf16[32,2,32,256]{3,2,1,0:T(8,128)(2,1)}, u32[]{:S(2)}, u32[]{:S(2)}) async-start(bf16[32,2,32,256]{3,2,1,0:T(8,128)(2,1)} %add_convert_fusion.2), calls=%async_computation.1 | async-start | bytes 2097152 | tf_op jit(solution)/shard_map/all_to_all | solution.py:142
  121.7 144.7 %all-reduce.15.cloned.1.call-start = ((), (), s32[]{:S(2)}) async-start(), calls=%async_computation.4 | async-start | bytes 3932160 | tf_op jit(solution)/shard_map/psum | solution.py:168
  127.1 1.0 copy-start.18
  127.1 1.0 copy-start.19
  266.4 5.0 %copy-start.15 = (f32[3,256,256]{2,1,0:T(8,128)S(1)}, f32[3,256,256]{2,1,0:T(8,128)}, u32[]{:S(2)}) copy-start(f32[3,256,256]{2,1,0:T(8,128)} %get-tuple-element.58) | copy-start | bytes 2359300
Sparse Core Ops, SparseCore 0:
  128.5 137.7 all-reduce.14
where the time goes:
time: 280 us; the launch traced here: 279 us
  waiting for transfers between devices  131 us (47%)
  blocking collectives  43.7 us (16%)
  starting transfers between devices  26.6 us (10%)
  matrix products  25.9 us (9%)
  local copies, waits for them, and re-layouts  25.6 us (9%)
  between operations  14.6 us (5%)
  other arithmetic  11.8 us (4%)
    psum x1, waiting for transfers between devices, per_device(): lax.psum((spatial_part, gain_partial_sum, bias_part, temporal_part), ('cl...  94.6 us
    psum x1, blocking collectives, per_device(): lax.psum((spatial_part, gain_partial_sum, bias_part, temporal_part), ('cl...  43.7 us
    all_to_all x1, waiting for transfers between devices, per_device(): lax.all_to_all(act_grad_rows, 'tm', split_axis=0, concat_axis=1, tiled=True)  14.2 us
    dot_general x9, matrix products, per_device(): jnp.dot(phases[row_phase, col_phase], spatial_weight[row_offset, col_offs...  11.5 us
    all_to_all x1, waiting for transfers between devices, per_device(): lax.all_to_all(acts, 'tm', split_axis=1, concat_axis=0, tiled=True)  11.3 us
    all_to_all x1, waiting for transfers between devices, per_device(): lax.all_to_all(upstream, 'tm', split_axis=1, concat_axis=0, tiled=True)  10.9 us
    unnamed x75, local copies, waits for them, and re-layouts  10.3 us
    all_to_all x1, starting transfers between devices, per_device(): lax.all_to_all(upstream, 'tm', split_axis=1, concat_axis=0, tiled=True)  8.36 us
  transfers between devices with their start and end apart: 5, of which 4 were waited for; matrix products, arithmetic and copies ran while one was open for 14% of the time, Pallas kernels for 0%

commit v1 on v0

--- a/solution.py
+++ b/solution.py
@@ -1,6 +1,10 @@
+import functools
+
 import jax
 import jax.numpy as jnp
 from jax import lax
+from jax.experimental import pallas as pl
+from jax.experimental.pallas import tpu as pltpu
 from jax.sharding import PartitionSpec as P
 
 GROUPS = 32
@@ -64,49 +68,109 @@
     return jax.nn.silu(normed * gain + bias)
 
 
-def padded_lag(values, frame_offset):
-    if frame_offset == 0:
-        return values
-    frames = values.shape[0]
-    if frame_offset > 0:
-        filler = jnp.zeros((frame_offset,) + values.shape[1:], values.dtype)
-        return jnp.concatenate([filler, values[: frames - frame_offset]], axis=0)
-    filler = jnp.zeros((-frame_offset,) + values.shape[1:], values.dtype)
-    return jnp.concatenate([values[-frame_offset:], filler], axis=0)
-
-
-def temporal_pass(acts, grads, weight, lag_rule):
-    chans = acts.shape[-1]
-    total = acts.astype(jnp.float32)
-    backward_total_sum = grads.astype(jnp.float32)
-    tap_grads = []
-    flattened_gradients = grads.reshape(-1, chans)
-    for kernel_tap_index in range(3):
-        frame_offset = kernel_tap_index * DILATION_FRAMES
-        earlier = lag_rule(acts, frame_offset).reshape(-1, chans)
-        later = lag_rule(grads, -frame_offset).reshape(-1, chans)
-        total = total + jnp.dot(
-            earlier, weight[kernel_tap_index], preferred_element_type=jnp.float32
-        ).reshape(acts.shape)
-        backward_total_sum = backward_total_sum + jnp.dot(
-            later, weight[kernel_tap_index].T, preferred_element_type=jnp.float32
-        ).reshape(acts.shape)
-        tap_grads.append(
-            lax.dot_general(
-                earlier,
-                flattened_gradients,
-                (((0,), (0,)), ((), ())),
-                preferred_element_type=jnp.float32,
-            )
-        )
-    return (
-        total.astype(jnp.bfloat16),
-        backward_total_sum.astype(jnp.bfloat16),
-        jnp.stack(tap_grads),
-    )
-
-
-def per_device(clip_frames, spatial_weight, norm_gain, norm_bias, temporal_weight, cotangent):
+def from_device(values, offset, tm_size):
+    pairs = [(src, src + offset) for src in range(tm_size) if 0 <= src + offset < tm_size]
+    return lax.ppermute(values, "tm", pairs)
+
+
+def bit_steps(clip_size, tm_size):
+    steps = [("clip", 1)] if clip_size > 1 else []
+    steps += [("tm", 1 << k) for k in range(tm_size.bit_length() - 1)]
+    steps += [("clip", 1 << k) for k in range(1, clip_size.bit_length() - 1)]
+    return steps
+
+
+def sum_kernel(steps, x_ref, out_ref, acc, outgoing, incoming, rs_send, rs_recv, ag_send, ag_recv):
+    place = {"clip": lax.axis_index("clip"), "tm": lax.axis_index("tm")}
+    bits, partners = [], []
+    for axis, weight in steps:
+        bit = (place[axis] // weight) % 2
+        other = place[axis] + weight * (1 - 2 * bit)
+        bits.append(bit)
+        partners.append((other, place["tm"]) if axis == "clip" else (place["clip"], other))
+
+    barrier = pltpu.get_barrier_semaphore()
+    for partner in partners:
+        pl.semaphore_signal(
+            barrier, inc=1, device_id=partner, device_id_type=pl.DeviceIdType.MESH
+        )
+    pl.semaphore_wait(barrier, len(partners))
+
+    base = 0
+    half = x_ref.shape[0] // 2
+    offset = 0
+    bases = []
+    copies = []
+    for step, partner in enumerate(partners):
+        source = x_ref if step == 0 else acc
+        keep = base + bits[step] * half
+        give = base + (1 - bits[step]) * half
+        slot = pl.ds(offset, half)
+        outgoing[slot] = source[pl.ds(give, half)].astype(jnp.bfloat16)
+        copy = pltpu.make_async_remote_copy(
+            src_ref=outgoing.at[slot],
+            dst_ref=incoming.at[slot],
+            send_sem=rs_send.at[step],
+            recv_sem=rs_recv.at[step],
+            device_id=partner,
+            device_id_type=pl.DeviceIdType.MESH,
+        )
+        copy.start()
+        copies.append(copy)
+        copy.wait_recv()
+        acc[pl.ds(keep, half)] = source[pl.ds(keep, half)] + incoming[slot].astype(jnp.float32)
+        bases.append(keep)
+        base = keep
+        offset += half
+        half //= 2
+
+    out_ref[pl.ds(base, 1)] = acc[pl.ds(base, 1)].astype(jnp.bfloat16)
+    size = 1
+    for step in reversed(range(len(partners))):
+        held = out_ref.at[pl.ds(bases[step], size)]
+        copy = pltpu.make_async_remote_copy(
+            src_ref=held,
+            dst_ref=held,
+            send_sem=ag_send.at[step],
+            recv_sem=ag_recv.at[step],
+            device_id=partners[step],
+            device_id_type=pl.DeviceIdType.MESH,
+        )
+        copy.start()
+        copies.append(copy)
+        copy.wait_recv()
+        size *= 2
+    for copy in copies:
+        copy.wait_send()
+
+
+def sum_everywhere(values, clip_size, tm_size):
+    devices = clip_size * tm_size
+    steps = bit_steps(clip_size, tm_size)
+    rows, chans = values.shape
+    unit = 8 * devices
+    padded = -(-rows // unit) * unit
+    values = jnp.pad(values, ((0, padded - rows), (0, 0)))
+    shape = (devices, padded // devices, chans)
+    total = pl.pallas_call(
+        functools.partial(sum_kernel, steps),
+        out_shape=jax.ShapeDtypeStruct(shape, jnp.bfloat16),
+        in_specs=[pl.BlockSpec(memory_space=pltpu.VMEM)],
+        out_specs=pl.BlockSpec(memory_space=pltpu.VMEM),
+        scratch_shapes=[
+            pltpu.VMEM(shape, jnp.float32),
+            pltpu.VMEM(shape, jnp.bfloat16),
+            pltpu.VMEM(shape, jnp.bfloat16),
+        ]
+        + [pltpu.SemaphoreType.DMA((len(steps),))] * 4,
+        compiler_params=pltpu.CompilerParams(
+            collective_id=0, has_side_effects=True, vmem_limit_bytes=32 * 1024 * 1024
+        ),
+    )(values.reshape(shape))
+    return total.astype(jnp.float32).reshape(padded, chans)[:rows]
+
+
+def per_device(clip_size, tm_size, clip_frames, spatial_weight, norm_gain, norm_bias, temporal_weight, cotangent):
     frames_in = clip_frames[0]
     upstream = cotangent[0]
     frames, height, width, _ = frames_in.shape
@@ -134,13 +198,29 @@
     conv_out = conv_out + delay_rows(delay_cols(partial_sums[True, True].reshape(out_shape)))
     activated, pullback = jax.vjp(activate, conv_out, norm_gain, norm_bias)
     acts = activated.astype(jnp.bfloat16)
-    act_rows = lax.all_to_all(acts, "tm", split_axis=1, concat_axis=0, tiled=True)
-    grad_rows = lax.all_to_all(upstream, "tm", split_axis=1, concat_axis=0, tiled=True)
-    mixed_rows, act_grad_rows, temporal_part = temporal_pass(
-        act_rows, grad_rows, temporal_weight, padded_lag
-    )
-    mixed = lax.all_to_all(mixed_rows, "tm", split_axis=0, concat_axis=1, tiled=True)
-    act_grad = lax.all_to_all(act_grad_rows, "tm", split_axis=0, concat_axis=1, tiled=True)
+    flat_acts = acts.reshape(-1, out_chans)
+    mixed_sum = flat_acts.astype(jnp.float32)
+    act_grad_sum = upstream.reshape(-1, out_chans).astype(jnp.float32)
+    tap_grads = []
+    for tap in range(3):
+        hop = tap * DILATION_FRAMES // frames
+        earlier = from_device(acts, hop, tm_size) if tap else acts
+        later = from_device(upstream, -hop, tm_size) if tap else upstream
+        earlier = earlier.reshape(-1, out_chans)
+        later = later.reshape(-1, out_chans)
+        mixed_sum = mixed_sum + jnp.dot(
+            earlier, temporal_weight[tap], preferred_element_type=jnp.float32
+        )
+        act_grad_sum = act_grad_sum + jnp.dot(
+            later, temporal_weight[tap].T, preferred_element_type=jnp.float32
+        )
+        tap_grads.append(
+            lax.dot_general(
+                flat_acts, later, (((0,), (0,)), ((), ())), preferred_element_type=jnp.float32
+            )
+        )
+    mixed = mixed_sum.astype(jnp.bfloat16).reshape(out_shape)
+    act_grad = act_grad_sum.astype(jnp.bfloat16).reshape(out_shape)
     conv_grad, gain_partial_sum, bias_part = pullback(act_grad.astype(jnp.float32))
     conv_grad = conv_grad.astype(jnp.bfloat16)
     grad_versions = {
@@ -149,13 +229,12 @@
         (False, True): advance_cols(conv_grad).reshape(-1, out_chans),
         (True, True): advance_rows(advance_cols(conv_grad)).reshape(-1, out_chans),
     }
-    tap_rows = []
+    parts = []
     for row_offset in range(3):
         row_phase, row_delay = tap_layout(row_offset)
-        tap_row = []
         for col_offset in range(3):
             col_phase, col_delay = tap_layout(col_offset)
-            tap_row.append(
+            parts.append(
                 lax.dot_general(
                     phases[row_phase, col_phase],
                     grad_versions[row_delay, col_delay],
@@ -163,17 +242,21 @@
                     preferred_element_type=jnp.float32,
                 )
             )
-        tap_rows.append(jnp.stack(tap_row))
-    spatial_part = jnp.stack(tap_rows)
-    spatial_gradient_total, gain_total, bias_total, temporal_total = lax.psum(
-        (spatial_part, gain_partial_sum, bias_part, temporal_part), ("clip", "tm")
+    spatial_rows = 9 * spatial_weight.shape[2]
+    parts += tap_grads + [gain_partial_sum[None], bias_part[None]]
+    totals = sum_everywhere(jnp.concatenate(parts), clip_size, tm_size)
+    spatial_gradient_total = totals[:spatial_rows].reshape(spatial_weight.shape)
+    temporal_total = totals[spatial_rows : spatial_rows + 3 * out_chans].reshape(
+        temporal_weight.shape
     )
+    gain_total = totals[spatial_rows + 3 * out_chans]
+    bias_total = totals[spatial_rows + 3 * out_chans + 1]
     return (mixed[None], spatial_gradient_total, gain_total, bias_total, temporal_total)
 
 
 def solution(mesh):
     return jax.shard_map(
-        per_device,
+        functools.partial(per_device, mesh.shape["clip"], mesh.shape["tm"]),
         mesh=mesh,
         in_specs=(
             P("clip", "tm", None, None, None),

time: 280 us -> 150 us (0.54)
  the two profiles are of different devices: /device:TPU:0 before, /device:TPU:21 now
where the time goes in v1:
time: 150 us; the launch traced here: 149 us
  Pallas kernels  58.8 us (39%)
  waiting for transfers between devices  29.8 us (20%)
  matrix products  26 us (17%)
  local copies, waits for them, and re-layouts  21.7 us (14%)
  starting transfers between devices  8.05 us (5%)
  other arithmetic  3.79 us (3%)
    pallas_call x1, Pallas kernels, sum_everywhere(): pl.pallas_call(functools.partial(sum_kernel, steps), out_shape=jax.ShapeD...  58.8 us
    ppermute x4, waiting for transfers between devices, from_device(): return lax.ppermute(values, 'tm', pairs)  29.8 us
    concatenate x1, local copies, waits for them, and re-layouts, per_device(): totals = sum_everywhere(jnp.concatenate(parts), clip_size, tm_size)  10.2 us
    dot_general x9, matrix products, per_device(): lax.dot_general(phases[row_phase, col_phase], grad_versions[row_delay, co...  8.47 us
    ppermute x4, starting transfers between devices, from_device(): return lax.ppermute(values, 'tm', pairs)  8.05 us
    slice x1, local copies, waits for them, and re-layouts, split_phases(): viewed[:, :, row_phase, :, col_phase, :].reshape(-1, chans)  6.34 us
    dot_general x3, matrix products, per_device(): jnp.dot(earlier, temporal_weight[tap], preferred_element_type=jnp.float32)  4.76 us
    dot_general x9, matrix products, per_device(): jnp.dot(phases[row_phase, col_phase], spatial_weight[row_offset, col_offs...  4.06 us
  transfers between devices with their start and end apart: 4, of which 2 were waited for; matrix products, arithmetic and copies ran while one was open for 23% of the time, Pallas kernels for 39%

profile of v1, /device:TPU:21, one launch (start us, length us, event | category | flops | bytes accessed | tf_op | source)
XLA Modules:
  0.0 149.0 jit_solution(9544094964776365944)
XLA Ops:
  0.6 2.1 %collective-permute-start.3 = (bf16[2,32,32,256]{3,2,1,0:T(8,128)(2,1)}, bf16[2,32,32,256]{3,2,1,0:T(8,128)(2,1)S(1)}, u32[]{:S(2)}, u32[]{:S(2)}) collective-permute-start(bf16[2,32,32,256]{3,2,1,0:T(8,128)(2,1)} %bitcast.192), channel_id=1, source_target_pairs={{4,0},{5,1},{6,2},{7,3},{8,4},{9,5},{10,6},{11,7},{12,8},{13,9},{1... | collective-permute-start | bytes 3145736 | tf_op jit(solution)/shard_map/ppermute | solution.py:73
  2.7 2.1 %collective-permute-start.2 = (bf16[2,32,32,256]{3,2,1,0:T(8,128)(2,1)}, bf16[2,32,32,256]{3,2,1,0:T(8,128)(2,1)S(1)}, u32[]{:S(2)}, u32[]{:S(2)}) collective-permute-start(bf16[2,32,32,256]{3,2,1,0:T(8,128)(2,1)} %bitcast.193), channel_id=1, source_target_pairs={{2,0},{3,1},{4,2},{5,3},{6,4},{7,5},{8,6},{9,7},{10,8},{11,9},{12,... | collective-permute-start | bytes 3145736 | tf_op jit(solution)/shard_map/ppermute | solution.py:73
  4.9 6.3 %fusion.84 = (bf16[2,32,1,32,1,128]{5,4,3,2,1,0:T(2,128)(2,1)S(1)}, bf16[2,32,1,32,1,128]{5,4,3,2,1,0:T(2,128)(2,1)S(1)}, bf16[2,32,1,32,1,128]{5,4,3,2,1,0:T(2,128)(2,1)S(1)}, bf16[2,32,1,32,1,128]{5,4,3,2,1,0:T(2,128)(2,1)S(1)}) fusion(bf16[2,32,2,32,2,128]{5,4,3,2,1,0:T(2,128)(2,1)} %bitcast.187), kind=kLoop, calls=%fused_computation.132 | loop fusion | bytes 4194304 | tf_op jit(solution)/shard_map/slice | solution.py:39
  11.5 0.9 copy-done.2
  12.3 0.4 fusion.42
  12.7 0.4 fusion.34
  13.2 0.4 convolution_add_fusion.8
  13.7 0.4 fusion.37
  14.1 0.4 convolution_add_fusion.7
  14.6 0.4 fusion.11
  15.0 0.4 convolution_add_fusion.4
  15.5 0.4 convolution_add_fusion.5
  16.2 0.7 fusion.81
  16.9 0.3 convolution_multiply_fusion.3
  17.5 0.3 multiply_reduce_fusion.2
  17.8 0.3 fusion.9
  18.4 0.5 convolution_add_fusion.1
  19.0 7.8 %collective-permute-done.3 = bf16[2,32,32,256]{3,2,1,0:T(8,128)(2,1)S(1)} collective-permute-done((bf16[2,32,32,256]{3,2,1,0:T(8,128)(2,1)}, bf16[2,32,32,256]{3,2,1,0:T(8,128)(2,1)S(1)}, u32[]{:S(2)}, u32[]{:S(2)}) %collective-permute-start.3) | collective-permute-done | bytes 1048608 | tf_op jit(solution)/shard_map/ppermute | solution.py:73
  26.8 0.5 fusion.14
  27.2 21.9 %collective-permute-done.2 = bf16[2,32,32,256]{3,2,1,0:T(8,128)(2,1)S(1)} collective-permute-done((bf16[2,32,32,256]{3,2,1,0:T(8,128)(2,1)}, bf16[2,32,32,256]{3,2,1,0:T(8,128)(2,1)S(1)}, u32[]{:S(2)}, u32[]{:S(2)}) %collective-permute-start.2) | collective-permute-done | bytes 1048608 | tf_op jit(solution)/shard_map/ppermute | solution.py:73
  49.2 1.9 %fusion.80 = (f32[256]{0:T(256)S(1)}, f32[256]{0:T(256)S(1)}, f32[2,256]{1,0:T(2,128)S(1)}, bf16[2048,256]{1,0:T(8,128)(2,1)S(1)}) fusion(f32[256]{0:T(256)S(1)} %copy-done.3, f32[256]{0:T(256)S(1)} %copy-done.4, f32[2,256]{1,0:T(2,128)S(1)} %fusion.24, f32[2,32,32,256]{3,2,1,0:T(8,128)S(1)} %get-tuple-element.9, f32[2,256]{1,0:T(2,128)S(1)} %fusion.25, ...), kind=kOutput, calls=%fused_computation.129 | convolution fusion | flops 280493056 | bytes 8529920 | tf_op jit(solution)/shard_map/dot_general | solution.py:214
  51.1 0.3 fusion.10
  51.6 1.5 %fusion.13 = f32[2,256]{1,0:T(2,128)S(1)} fusion(f32[2,256]{1,0:T(2,128)S(1)} %fusion.23, f32[2,32,32,256]{3,2,1,0:T(8,128)S(1)} %get-tuple-element.9, f32[2,256]{1,0:T(2,128)S(1)} %fusion.25, f32[2,256]{1,0:T(2,128)S(1)} %fusion.24, f32[256]{0:T(256)S(1)} %copy-done.4, f32[256]{0:T(256)S(1)} %copy-done.3, bf16[2048,256]{1,0:T(8,128)(2,1)S(1)} %get-tuple-element.20), kind=kLoop, calls=%fused_computation.55 | loop fusion | flops 10485248 | bytes 3155968 | tf_op jit(solution)/shard_map/transpose(jvp())/reduce_sum | solution.py:63
  53.2 0.3 convolution_multiply_fusion
  53.7 1.7 %add_convert_fusion = (bf16[2,32,32,256]{3,2,1,0:T(8,128)(2,1)S(1)}, bf16[2,32,32,256]{3,2,1,0:T(8,128)(2,1)S(1)}) fusion(f32[2,256]{1,0:T(2,128)S(1)} %fusion.22, f32[2,256]{1,0:T(2,128)S(1)} %fusion.23, f32[2,32,32,256]{3,2,1,0:T(8,128)S(1)} %get-tuple-element.9, f32[2,256]{1,0:T(2,128)S(1)} %fusion.25, f32[2,256]{1,0:T(2,128)S(1)} %fusion.24, ...), kind=kLoop, calls=%fused_computation.27 | loop fusion | flops 12058624 | bytes 5253120 | tf_op jit(solution)/shard_map/convert_element_type | solution.py:225
  55.5 0.7 pad_slice_fusion.5
  56.3 0.3 convolution_bitcast_fusion.4
  56.6 1.1 convolution_bitcast_fusion.7
  57.7 1.0 convolution_bitcast_fusion.8
  58.7 1.0 convolution_bitcast_fusion.9
  59.7 1.0 convolution_bitcast_fusion.2
  60.7 1.0 convolution_bitcast_fusion.3
  61.7 1.0 convolution_bitcast_fusion.5
  62.7 1.9 %collective-permute-start.1 = (bf16[2,32,32,256]{3,2,1,0:T(8,128)(2,1)S(1)}, bf16[2,32,32,256]{3,2,1,0:T(8,128)(2,1)}, u32[]{:S(2)}, u32[]{:S(2)}) collective-permute-start(bf16[2,32,32,256]{3,2,1,0:T(8,128)(2,1)S(1)} %get-tuple-element.11), channel_id=1, source_target_pairs={{0,4},{1,5},{2,6},{3,7},{4,8},{5,9},{6,10},{7,11},{8,12},{9,13},{1... | collective-permute-start | bytes 3145736 | tf_op jit(solution)/shard_map/ppermute | solution.py:73
  64.7 1.9 %collective-permute-start = (bf16[2,32,32,256]{3,2,1,0:T(8,128)(2,1)S(1)}, bf16[2,32,32,256]{3,2,1,0:T(8,128)(2,1)}, u32[]{:S(2)}, u32[]{:S(2)}) collective-permute-start(bf16[2,32,32,256]{3,2,1,0:T(8,128)(2,1)S(1)} %get-tuple-element.11), channel_id=1, source_target_pairs={{0,2},{1,3},{2,4},{3,5},{4,6},{5,7},{6,8},{7,9},{8,10},{9,11},{10,... | collective-permute-start | bytes 3145736 | tf_op jit(solution)/shard_map/ppermute | solution.py:73
  66.6 1.2 fusion.85
  67.8 1.2 convolution_bitcast_fusion
  68.9 1.2 convolution_bitcast_fusion.1
  70.1 1.0 convolution_bitcast_fusion.6
  71.1 1.0 convolution_bitcast_fusion.10
  72.1 10.2 %concatenate.3 = f32[1922,256]{1,0:T(8,128)S(1)} concatenate(f32[128,256]{1,0:T(8,128)} %convolution_bitcast_fusion.10, f32[128,256]{1,0:T(8,128)} %convolution_bitcast_fusion.9, f32[128,256]{1,0:T(8,128)} %convolution_bitcast_fusion.8, f32[128,256]{1,0:T(8,128)} %convolution_bitcast_fusion.7, f32[128,256]{1,0:T(8,128)} %convolution_bitcast_fusion.6, ...), dimensions={0} | concatenate | bytes 3936256 | tf_op jit(solution)/shard_map/concatenate | solution.py:247
  82.5 58.8 %shard_map.101 = bf16[32,64,256]{2,1,0:T(8,128)(2,1)S(1)} custom-call(f32[32,64,256]{2,1,0:T(8,128)S(1)} %bitcast.161), custom_call_target="tpu_custom_call" | custom-call | tf_op jit(solution)/shard_map/pallas_call | solution.py:155
  141.6 1.2 slice.123
  142.7 1.0 slice.126
  143.7 0.6 fusion.83
  144.2 0.4 convolution_add_fusion.3
  144.7 1.7 %fusion.16 = f32[2048,256]{1,0:T(8,128)S(1)} fusion(bf16[2048,256]{1,0:T(8,128)(2,1)} %bitcast.21, bf16[3,256,256]{2,1,0:T(8,128)(2,1)S(1)} %copy-done.1), kind=kOutput, calls=%fused_computation.58 | convolution fusion | flops 268435456 | bytes 3276800 | tf_op jit(solution)/shard_map/dot_general | solution.py:211
  146.3 2.7 %fusion.2 = bf16[2048,256]{1,0:T(8,128)(2,1)} fusion(f32[2048,256]{1,0:T(8,128)S(1)} %fusion.16, f32[2048,256]{1,0:T(8,128)S(1)} %convolution_add_fusion.3, bf16[2048,256]{1,0:T(8,128)(2,1)} %bitcast.19, bf16[3,256,256]{2,1,0:T(8,128)(2,1)S(1)} %copy-done.1), kind=kOutput, calls=%fused_computation.17 | convolution fusion | flops 270008320 | bytes 6422528 | tf_op jit(solution)/shard_map/dot_general | solution.py:211
  (26 shorter events, 2.3 us)
Async XLA Ops:
  0.6 26.1 %collective-permute-start.3 = (bf16[2,32,32,256]{3,2,1,0:T(8,128)(2,1)}, bf16[2,32,32,256]{3,2,1,0:T(8,128)(2,1)S(1)}, u32[]{:S(2)}, u32[]{:S(2)}) collective-permute-start(bf16[2,32,32,256]{3,2,1,0:T(8,128)(2,1)} %bitcast.192), channel_id=1, source_target_pairs={{4,0},{5,1},{6,2},{7,3},{8,4},{9,5},{10,6},{11,7},{12,8},{13,9},{1... | collective-permute-start | bytes 3145736 | tf_op jit(solution)/shard_map/ppermute | solution.py:73
  2.7 46.5 %collective-permute-start.2 = (bf16[2,32,32,256]{3,2,1,0:T(8,128)(2,1)}, bf16[2,32,32,256]{3,2,1,0:T(8,128)(2,1)S(1)}, u32[]{:S(2)}, u32[]{:S(2)}) collective-permute-start(bf16[2,32,32,256]{3,2,1,0:T(8,128)(2,1)} %bitcast.193), channel_id=1, source_target_pairs={{2,0},{3,1},{4,2},{5,3},{6,4},{7,5},{8,6},{9,7},{10,8},{11,9},{12,... | collective-permute-start | bytes 3145736 | tf_op jit(solution)/shard_map/ppermute | solution.py:73
  11.2 1.1 copy-start.2
  16.9 1.5 copy-start
  16.9 1.5 %copy-start.1 = (bf16[3,256,256]{2,1,0:T(8,128)(2,1)S(1)}, bf16[3,256,256]{2,1,0:T(8,128)(2,1)}, u32[]{:S(2)}) copy-start(bf16[3,256,256]{2,1,0:T(8,128)(2,1)} %param.10) | copy-start | bytes 1179652
  18.9 30.2 %copy-start.3 = (f32[256]{0:T(256)S(1)}, f32[256]{0:T(256)}, u32[]{:S(2)}) copy-start(f32[256]{0:T(256)} %param.9) | copy-start | bytes 3076
  18.9 30.2 %copy-start.4 = (f32[256]{0:T(256)S(1)}, f32[256]{0:T(256)}, u32[]{:S(2)}) copy-start(f32[256]{0:T(256)} %param.8) | copy-start | bytes 3076
  62.7 81.9 %collective-permute-start.1 = (bf16[2,32,32,256]{3,2,1,0:T(8,128)(2,1)S(1)}, bf16[2,32,32,256]{3,2,1,0:T(8,128)(2,1)}, u32[]{:S(2)}, u32[]{:S(2)}) collective-permute-start(bf16[2,32,32,256]{3,2,1,0:T(8,128)(2,1)S(1)} %get-tuple-element.11), channel_id=1, source_target_pairs={{0,4},{1,5},{2,6},{3,7},{4,8},{5,9},{6,10},{7,11},{8,12},{9,13},{1... | collective-permute-start | bytes 3145736 | tf_op jit(solution)/shard_map/ppermute | solution.py:73
  64.7 81.7 %collective-permute-start = (bf16[2,32,32,256]{3,2,1,0:T(8,128)(2,1)S(1)}, bf16[2,32,32,256]{3,2,1,0:T(8,128)(2,1)}, u32[]{:S(2)}, u32[]{:S(2)}) collective-permute-start(bf16[2,32,32,256]{3,2,1,0:T(8,128)(2,1)S(1)} %get-tuple-element.11), channel_id=1, source_target_pairs={{0,2},{1,3},{2,4},{3,5},{4,6},{5,7},{6,8},{7,9},{8,10},{9,11},{10,... | collective-permute-start | bytes 3145736 | tf_op jit(solution)/shard_map/ppermute | solution.py:73

commit v2 on v1

--- a/solution.py
+++ b/solution.py
@@ -80,7 +80,12 @@
     return steps
 
 
-def sum_kernel(steps, x_ref, out_ref, acc, outgoing, incoming, rs_send, rs_recv, ag_send, ag_recv):
+STREAMS = 2
+
+
+def sum_kernel(steps, sizes, *refs):
+    parts, refs = refs[: len(sizes)], refs[len(sizes) :]
+    out_ref, acc, outgoing, incoming, rs_send, rs_recv, ag_send, ag_recv = refs
     place = {"clip": lax.axis_index("clip"), "tm": lax.axis_index("tm")}
     bits, partners = [], []
     for axis, weight in steps:
@@ -94,80 +99,121 @@
         pl.semaphore_signal(
             barrier, inc=1, device_id=partner, device_id_type=pl.DeviceIdType.MESH
         )
+
+    _, devices, unit, chans = acc.shape
+    flat = acc.reshape(STREAMS * devices * unit, chans)
+    row = 0
+    for part, size in zip(parts, sizes):
+        flat[row : row + size] = part[...].reshape(size, chans)
+        row += size
+    flat[row:] = jnp.zeros((flat.shape[0] - row, chans), jnp.float32)
     pl.semaphore_wait(barrier, len(partners))
 
-    base = 0
-    half = x_ref.shape[0] // 2
-    offset = 0
-    bases = []
+    count = len(steps)
+    orders = [list(range(count)) for _ in range(STREAMS)]
+    if count > 2:
+        orders[1][1], orders[1][2] = 2, 1
+    base = [0] * STREAMS
+    kept = [[] for _ in range(STREAMS)]
+    flying = [None] * STREAMS
     copies = []
-    for step, partner in enumerate(partners):
-        source = x_ref if step == 0 else acc
-        keep = base + bits[step] * half
-        give = base + (1 - bits[step]) * half
-        slot = pl.ds(offset, half)
-        outgoing[slot] = source[pl.ds(give, half)].astype(jnp.bfloat16)
+
+    def send_half(stream, turn):
+        which = orders[stream][turn]
+        half = devices >> (turn + 1)
+        slot = pl.ds(devices - 2 * half, half)
+        give = base[stream] + (1 - bits[which]) * half
+        outgoing[stream, slot] = acc[stream, pl.ds(give, half)].astype(jnp.bfloat16)
         copy = pltpu.make_async_remote_copy(
-            src_ref=outgoing.at[slot],
-            dst_ref=incoming.at[slot],
-            send_sem=rs_send.at[step],
-            recv_sem=rs_recv.at[step],
-            device_id=partner,
+            src_ref=outgoing.at[stream, slot],
+            dst_ref=incoming.at[stream, slot],
+            send_sem=rs_send.at[stream, turn],
+            recv_sem=rs_recv.at[stream, turn],
+            device_id=partners[which],
             device_id_type=pl.DeviceIdType.MESH,
         )
         copy.start()
         copies.append(copy)
-        copy.wait_recv()
-        acc[pl.ds(keep, half)] = source[pl.ds(keep, half)] + incoming[slot].astype(jnp.float32)
-        bases.append(keep)
-        base = keep
-        offset += half
-        half //= 2
-
-    out_ref[pl.ds(base, 1)] = acc[pl.ds(base, 1)].astype(jnp.bfloat16)
-    size = 1
-    for step in reversed(range(len(partners))):
-        held = out_ref.at[pl.ds(bases[step], size)]
+        flying[stream] = copy
+
+    def add_half(stream, turn):
+        which = orders[stream][turn]
+        half = devices >> (turn + 1)
+        slot = pl.ds(devices - 2 * half, half)
+        keep = base[stream] + bits[which] * half
+        flying[stream].wait_recv()
+        acc[stream, pl.ds(keep, half)] += incoming[stream, slot].astype(jnp.float32)
+        kept[stream].append(keep)
+        base[stream] = keep
+
+    def send_held(stream, turn):
+        which = orders[stream][turn]
+        held = out_ref.at[stream, pl.ds(kept[stream][turn], devices >> (turn + 1))]
         copy = pltpu.make_async_remote_copy(
             src_ref=held,
             dst_ref=held,
-            send_sem=ag_send.at[step],
-            recv_sem=ag_recv.at[step],
-            device_id=partners[step],
+            send_sem=ag_send.at[stream, turn],
+            recv_sem=ag_recv.at[stream, turn],
+            device_id=partners[which],
             device_id_type=pl.DeviceIdType.MESH,
         )
         copy.start()
         copies.append(copy)
-        copy.wait_recv()
-        size *= 2
+        flying[stream] = copy
+
+    for stream in range(STREAMS):
+        send_half(stream, 0)
+    for turn in range(count):
+        for stream in range(STREAMS):
+            add_half(stream, turn)
+            if turn + 1 < count:
+                send_half(stream, turn + 1)
+            else:
+                own = pl.ds(base[stream], 1)
+                out_ref[stream, own] = acc[stream, own].astype(jnp.bfloat16)
+                send_held(stream, turn)
+    for turn in reversed(range(count)):
+        for stream in range(STREAMS):
+            flying[stream].wait_recv()
+            if turn > 0:
+                send_held(stream, turn - 1)
     for copy in copies:
         copy.wait_send()
 
 
-def sum_everywhere(values, clip_size, tm_size):
+def sum_everywhere(parts, clip_size, tm_size):
     devices = clip_size * tm_size
     steps = bit_steps(clip_size, tm_size)
-    rows, chans = values.shape
-    unit = 8 * devices
-    padded = -(-rows // unit) * unit
-    values = jnp.pad(values, ((0, padded - rows), (0, 0)))
-    shape = (devices, padded // devices, chans)
+    chans = parts[0].shape[-1]
+    sizes = tuple(part.shape[0] for part in parts)
+    unit = -(-sum(sizes) // (STREAMS * devices * 8)) * 8
+    shape = (STREAMS, devices, unit, chans)
     total = pl.pallas_call(
-        functools.partial(sum_kernel, steps),
+        functools.partial(sum_kernel, steps, sizes),
         out_shape=jax.ShapeDtypeStruct(shape, jnp.bfloat16),
-        in_specs=[pl.BlockSpec(memory_space=pltpu.VMEM)],
+        in_specs=[pl.BlockSpec(memory_space=pltpu.VMEM)] * len(parts),
         out_specs=pl.BlockSpec(memory_space=pltpu.VMEM),
         scratch_shapes=[
             pltpu.VMEM(shape, jnp.float32),
             pltpu.VMEM(shape, jnp.bfloat16),
             pltpu.VMEM(shape, jnp.bfloat16),
         ]
-        + [pltpu.SemaphoreType.DMA((len(steps),))] * 4,
+        + [pltpu.SemaphoreType.DMA((STREAMS, len(steps)))] * 4,
         compiler_params=pltpu.CompilerParams(
             collective_id=0, has_side_effects=True, vmem_limit_bytes=32 * 1024 * 1024
         ),
-    )(values.reshape(shape))
-    return total.astype(jnp.float32).reshape(padded, chans)[:rows]
+    )(*parts)
+    return total.reshape(-1, chans).astype(jnp.float32)
+
+
+def later_frames(upstream, hop, tm_size):
+    upper = (lax.axis_index("tm") // hop) % 2 == 1
+    lows = [place for place in range(tm_size) if place // hop % 2 == 0]
+    far = [from_device(block, -2 * hop, tm_size) for block in upstream]
+    own = lax.ppermute(upstream, "tm", [(low + hop, low) for low in lows])
+    passed = [lax.ppermute(block, "tm", [(low, low + hop) for low in lows]) for block in far]
+    near = [jnp.where(upper, passed[k], own[k]) for k in range(len(far))]
+    return jnp.stack(near), jnp.stack(far)
 
 
 def per_device(clip_size, tm_size, clip_frames, spatial_weight, norm_gain, norm_bias, temporal_weight, cotangent):
@@ -202,10 +248,17 @@
     mixed_sum = flat_acts.astype(jnp.float32)
     act_grad_sum = upstream.reshape(-1, out_chans).astype(jnp.float32)
     tap_grads = []
+    hop = DILATION_FRAMES // frames
+    near, far = later_frames(upstream, hop, tm_size)
+    far_acts = from_device(acts, 2 * hop, tm_size)
+    upstream, near, far, far_acts = lax.optimization_barrier((upstream, near, far, far_acts))
+    upper = (lax.axis_index("tm") // hop) % 2 == 1
+    near_acts = lax.ppermute(
+        jnp.where(upper, far_acts, acts), "tm", [(src, src ^ hop) for src in range(tm_size)]
+    )
     for tap in range(3):
-        hop = tap * DILATION_FRAMES // frames
-        earlier = from_device(acts, hop, tm_size) if tap else acts
-        later = from_device(upstream, -hop, tm_size) if tap else upstream
+        earlier = (acts, near_acts, far_acts)[tap]
+        later = (upstream, near, far)[tap]
         earlier = earlier.reshape(-1, out_chans)
         later = later.reshape(-1, out_chans)
         mixed_sum = mixed_sum + jnp.dot(
@@ -243,8 +296,9 @@
                 )
             )
     spatial_rows = 9 * spatial_weight.shape[2]
-    parts += tap_grads + [gain_partial_sum[None], bias_part[None]]
-    totals = sum_everywhere(jnp.concatenate(parts), clip_size, tm_size)
+    parts += tap_grads
+    parts.append(jnp.stack([gain_partial_sum, bias_part]))
+    totals = sum_everywhere(parts, clip_size, tm_size)
     spatial_gradient_total = totals[:spatial_rows].reshape(spatial_weight.shape)
     temporal_total = totals[spatial_rows : spatial_rows + 3 * out_chans].reshape(
         temporal_weight.shape

time: 150 us -> 136 us (0.907)
  the two profiles are of different devices: /device:TPU:21 before, /device:TPU:0 now
where the time goes in v2:
time: 136 us
  Pallas kernels  50.3 us (37%)
  matrix products  24.3 us (18%)
  starting transfers between devices  23.6 us (17%)
  waiting for transfers between devices  16 us (12%)
  local copies, waits for them, and re-layouts  11.6 us (9%)
  other arithmetic  8.84 us (6%)
    pallas_call x1, Pallas kernels, sum_everywhere(): pl.pallas_call(functools.partial(sum_kernel, steps, sizes), out_shape=jax...  50.3 us
    ppermute x2, waiting for transfers between devices, later_frames(): lax.ppermute(block, 'tm', [(low, low + hop) for low in lows])  16 us
    ppermute x3, starting transfers between devices, from_device(): return lax.ppermute(values, 'tm', pairs)  9.76 us
    ppermute x2, starting transfers between devices, later_frames(): lax.ppermute(block, 'tm', [(low, low + hop) for low in lows])  8.42 us
    dot_general x3, matrix products, per_device(): lax.dot_general(flat_acts, later, (((0,), (0,)), ((), ())), preferred_ele...  5.4 us
    dot_general x3, matrix products, per_device(): jnp.dot(earlier, temporal_weight[tap], preferred_element_type=jnp.float32)  5.15 us
    slice x1, local copies, waits for them, and re-layouts, split_phases(): viewed[:, :, row_phase, :, col_phase, :].reshape(-1, chans)  4.45 us
    dot_general x3, matrix products, per_device(): jnp.dot(later, temporal_weight[tap].T, preferred_element_type=jnp.float32)  4.29 us
  transfers between devices with their start and end apart: 7, of which 2 were waited for; matrix products, arithmetic and copies ran while one was open for 16% of the time, Pallas kernels for 37%

profile of v2, /device:TPU:0, one launch (start us, length us, event | category | flops | bytes accessed | tf_op | source)
XLA Modules:
  0.0 135.7 jit_solution(15880496740056831706)
XLA Ops:
  0.6 1.4 %slice_bitcast_fusion.3 = (bf16[32,32,256]{2,1,0:T(8,128)(2,1)S(1)}, bf16[32,32,256]{2,1,0:T(8,128)(2,1)S(1)}) fusion(bf16[1,2,32,32,256]{4,3,2,1,0:T(8,128)(2,1)} %param.11), kind=kLoop, calls=%fused_computation.67 | loop fusion | bytes 2097152 | tf_op jit(solution)/shard_map/unstack | solution.py:212
  2.1 1.3 collective-permute-start
  3.4 1.3 collective-permute-start.3
  4.7 1.3 collective-permute-start.2
  6.0 4.5 %fusion.86 = (bf16[2,32,1,32,1,128]{5,4,3,2,1,0:T(2,128)(2,1)S(1)}, bf16[2,32,1,32,1,128]{5,4,3,2,1,0:T(2,128)(2,1)S(1)}, bf16[2,32,1,32,1,128]{5,4,3,2,1,0:T(2,128)(2,1)S(1)}, bf16[2,32,1,32,1,128]{5,4,3,2,1,0:T(2,128)(2,1)S(1)}) fusion(bf16[2,32,2,32,2,128]{5,4,3,2,1,0:T(2,128)(2,1)S(1)} %bitcast.215), kind=kLoop, calls=%fused_computation.145 | loop fusion | bytes 4194304 | tf_op jit(solution)/shard_map/slice | solution.py:39
  10.7 0.8 copy-done.6
  11.6 0.4 fusion.44
  12.0 0.4 fusion.36
  12.4 0.4 convolution_add_fusion.9
  12.9 0.4 fusion.39
  13.3 0.4 convolution_add_fusion.8
  13.9 0.4 fusion.14
  14.3 0.4 convolution_add_fusion.5
  14.7 0.4 convolution_add_fusion.6
  15.1 0.5 pad_slice_fusion
  15.6 0.6 fusion.83
  17.5 0.6 copy-done.15
  18.3 1.7 %multiply_convert_fusion = bf16[2,32,32,256]{3,2,1,0:T(8,128)(2,1)} fusion(f32[2,32,32,256]{3,2,1,0:T(8,128)S(1)} %get-tuple-element.17, f32[256]{0:T(256)S(1)} %copy-done.7, f32[256]{0:T(256)S(1)} %copy-done.8, f32[2,256]{1,0:T(2,128)S(1)} %fusion.26, f32[2,256]{1,0:T(2,128)S(1)} %fusion.27), kind=kLoop, calls=%fused_computation.29 | loop fusion | flops 4718592 | bytes 3151872 | tf_op jit(solution)/shard_map/convert_element_type | solution.py:246
  20.0 7.2 %collective-permute-start.5 = (bf16[2,32,32,256]{3,2,1,0:T(8,128)(2,1)}, bf16[2,32,32,256]{3,2,1,0:T(8,128)(2,1)}, u32[]{:S(2)}, u32[]{:S(2)}) collective-permute-start(bf16[2,32,32,256]{3,2,1,0:T(8,128)(2,1)} %multiply_convert_fusion), channel_id=1, source_target_pairs={{0,4},{1,5},{2,6},{3,7},{4,8},{5,9},{6,10},{7,11},{8,12},{9,13},{1... | collective-permute-start | bytes 3145736 | tf_op jit(solution)/shard_map/ppermute | solution.py:73
  27.2 6.3 %collective-permute-start.1 = (bf16[32,32,256]{2,1,0:T(8,128)(2,1)}, bf16[32,32,256]{2,1,0:T(8,128)(2,1)}, u32[]{:S(2)}, u32[]{:S(2)}) collective-permute-start(bf16[32,32,256]{2,1,0:T(8,128)(2,1)} %collective-permute-done), channel_id=1, source_target_pairs={{0,2},{1,3},{4,6},{5,7},{8,10},{9,11},{12,14},{13,15},{16,18},{17,... | collective-permute-start | bytes 1572872 | tf_op jit(solution)/shard_map/ppermute | solution.py:214
  33.5 2.1 %collective-permute-start.4 = (bf16[32,32,256]{2,1,0:T(8,128)(2,1)}, bf16[32,32,256]{2,1,0:T(8,128)(2,1)}, u32[]{:S(2)}, u32[]{:S(2)}) collective-permute-start(bf16[32,32,256]{2,1,0:T(8,128)(2,1)} %collective-permute-done.3), channel_id=1, source_target_pairs={{0,2},{1,3},{4,6},{5,7},{8,10},{9,11},{12,14},{13,15},{16,18},{17,... | collective-permute-start | bytes 1572872 | tf_op jit(solution)/shard_map/ppermute | solution.py:214
  35.6 2.0 %convolution_add_fusion.4 = f32[2048,256]{1,0:T(8,128)S(1)} fusion(bf16[2048,256]{1,0:T(8,128)(2,1)} %bitcast.17, bf16[3,256,256]{2,1,0:T(8,128)(2,1)S(1)} %copy-done.5), kind=kOutput, calls=%fused_computation.7 | convolution fusion | flops 269484032 | bytes 4325376 | tf_op jit(solution)/shard_map/dot_general | solution.py:264
  37.6 1.3 pad_maximum_fusion.1
  38.9 6.5 %collective-permute-done.1 = bf16[32,32,256]{2,1,0:T(8,128)(2,1)} collective-permute-done((bf16[32,32,256]{2,1,0:T(8,128)(2,1)}, bf16[32,32,256]{2,1,0:T(8,128)(2,1)}, u32[]{:S(2)}, u32[]{:S(2)}) %collective-permute-start.1) | collective-permute-done | bytes 524320 | tf_op jit(solution)/shard_map/ppermute | solution.py:214
  45.4 9.4 %collective-permute-done.4 = bf16[32,32,256]{2,1,0:T(8,128)(2,1)} collective-permute-done((bf16[32,32,256]{2,1,0:T(8,128)(2,1)}, bf16[32,32,256]{2,1,0:T(8,128)(2,1)}, u32[]{:S(2)}, u32[]{:S(2)}) %collective-permute-start.4) | collective-permute-done | bytes 524320 | tf_op jit(solution)/shard_map/ppermute | solution.py:214
  54.8 1.3 fusion.13
  56.3 1.7 %convolution_bitcast_fusion.refs_11_ = f32[256,256]{1,0:T(8,128)S(1)} fusion(bf16[2,32,32,256]{3,2,1,0:T(8,128)(2,1)} %multiply_convert_fusion, bf16[2,32,32,256]{3,2,1,0:T(8,128)(2,1)S(1)} %pad_maximum_fusion.1), kind=kOutput, calls=%fused_computation.34 | convolution fusion | flops 268435456 | bytes 2359296 | tf_op jit(solution)/shard_map/dot_general | solution.py:271
  58.0 1.7 %convolution_bitcast_fusion.1.refs_10_ = f32[256,256]{1,0:T(8,128)S(1)} fusion(bf16[2,32,32,256]{3,2,1,0:T(8,128)(2,1)} %multiply_convert_fusion, bf16[2,32,32,256]{3,2,1,0:T(8,128)(2,1)S(1)} %pad_maximum_fusion), kind=kOutput, calls=%fused_computation.35 | convolution fusion | flops 268435456 | bytes 2359296 | tf_op jit(solution)/shard_map/dot_general | solution.py:271
  59.7 2.0 %convolution_bitcast_fusion.2.refs_9_ = f32[256,256]{1,0:T(8,128)S(1)} fusion(bf16[2,32,32,256]{3,2,1,0:T(8,128)(2,1)} %multiply_convert_fusion, bf16[2,32,32,256]{3,2,1,0:T(8,128)(2,1)} %bitcast.19), kind=kOutput, calls=%fused_computation.36 | convolution fusion | flops 268435456 | bytes 2359296 | tf_op jit(solution)/shard_map/dot_general | solution.py:271
  61.7 2.1 %convolution_add_fusion.2 = f32[2048,256]{1,0:T(8,128)S(1)} fusion(bf16[2048,256]{1,0:T(8,128)(2,1)} %bitcast.34, bf16[2048,256]{1,0:T(8,128)(2,1)} %bitcast.68, bf16[3,256,256]{2,1,0:T(8,128)(2,1)S(1)} %copy-done.5), kind=kOutput, calls=%fused_computation.4 | convolution fusion | flops 269484032 | bytes 4325376 | tf_op jit(solution)/shard_map/dot_general | solution.py:267
  63.8 0.5 convolution_add_fusion.1
  64.3 1.8 %multiply_reduce_fusion = (f32[256]{0:T(256)S(1)}, f32[256]{0:T(256)S(1)}, f32[2,256]{1,0:T(2,128)S(1)}, bf16[2048,256]{1,0:T(8,128)(2,1)S(1)}) fusion(f32[2,32,32,256]{3,2,1,0:T(8,128)S(1)} %get-tuple-element.17, f32[2,256]{1,0:T(2,128)S(1)} %fusion.26, f32[2,256]{1,0:T(2,128)S(1)} %fusion.27, f32[256]{0:T(256)S(1)} %copy-done.7, f32[256]{0:T(256)S(1)} %copy-done.8, ...), kind=kOutput, calls=%fused_computation.26 | convolution fusion | flops 279968768 | bytes 6432768 | tf_op jit(solution)/shard_map/dot_general | solution.py:267
  66.7 1.5 %fusion.16 = f32[2,256]{1,0:T(2,128)S(1)} fusion(f32[2,256]{1,0:T(2,128)S(1)} %fusion.25, f32[2,32,32,256]{3,2,1,0:T(8,128)S(1)} %get-tuple-element.17, f32[2,256]{1,0:T(2,128)S(1)} %fusion.27, f32[2,256]{1,0:T(2,128)S(1)} %fusion.26, f32[256]{0:T(256)S(1)} %copy-done.8, f32[256]{0:T(256)S(1)} %copy-done.7, bf16[2048,256]{1,0:T(8,128)(2,1)S(1)} %get-tuple-element.30), kind=kLoop, calls=%fused_computation.68 | loop fusion | flops 10485248 | bytes 3155968 | tf_op jit(solution)/shard_map/transpose(jvp())/reduce_sum | solution.py:63
  68.8 1.6 %add_convert_fusion = bf16[2,32,32,256]{3,2,1,0:T(8,128)(2,1)S(1)} fusion(f32[2,256]{1,0:T(2,128)S(1)} %fusion.24, f32[2,256]{1,0:T(2,128)S(1)} %fusion.25, f32[2,32,32,256]{3,2,1,0:T(8,128)S(1)} %get-tuple-element.17, f32[2,256]{1,0:T(2,128)S(1)} %fusion.27, f32[2,256]{1,0:T(2,128)S(1)} %fusion.26, f32[256]{0:T(256)S(1)} %copy-done.8, f32[256]{0:T(256)S(1)} %copy-done.7, ...), kind=kLoop, calls=%fused_computation.27 | loop fusion | flops 11010048 | bytes 4204544 | tf_op jit(solution)/shard_map/convert_element_type | solution.py:278
  70.4 0.4 convolution_bitcast_fusion.3.refs_8_
  71.1 0.7 pad_slice_fusion.5
  71.8 0.4 convolution_bitcast_fusion.6.refs_5_
  72.2 0.4 convolution_bitcast_fusion.7.refs_4_
  72.6 0.4 convolution_bitcast_fusion.5.refs_6_
  73.3 0.4 convolution_bitcast_fusion.9.refs_2_
  74.5 0.8 broadcast_select_fusion
  75.3 4.1 %collective-permute-start.6 = (bf16[2,32,32,256]{3,2,1,0:T(8,128)(2,1)S(1)}, bf16[2,32,32,256]{3,2,1,0:T(8,128)(2,1)S(1)}, u32[]{:S(2)}, u32[]{:S(2)}) collective-permute-start(bf16[2,32,32,256]{3,2,1,0:T(8,128)(2,1)S(1)} %broadcast_select_fusion), channel_id=1, source_target_pairs={{0,2},{1,3},{2,0},{3,1},{4,6},{5,7},{6,4},{7,5},{8,10},{9,11},{10,... | collective-permute-start | bytes 3145736 | tf_op jit(solution)/shard_map/ppermute | solution.py:256
  79.4 50.3 %shard_map.101 = bf16[2,32,32,256]{3,2,1,0:T(8,128)(2,1)S(1)} custom-call(f32[128,256]{1,0:T(8,128)S(1)} %convolution_bitcast_fusion.11.refs_0_, f32[128,256]{1,0:T(8,128)S(1)} %convolution_bitcast_fusion.10.refs_1_, f32[128,256]{1,0:T(8,128)S(1)} %convolution_bitcast_fusion.9.refs_2_, f32[128,256]{1,0:T(8,128)S(1)} %convolution_bitcast_fusion.8.refs_3_, ...), custom_call_target="tpu_custom_call" | custom-call | tf_op jit(solution)/shard_map/pallas_call | solution.py:191
  129.9 1.1 slice.128
  131.0 0.9 slice.131
  131.9 0.6 fusion.85
  132.5 1.6 %fusion.18 = f32[2048,256]{1,0:T(8,128)S(1)} fusion(bf16[2048,256]{1,0:T(8,128)(2,1)} %bitcast.30, bf16[3,256,256]{2,1,0:T(8,128)(2,1)S(1)} %copy-done.5), kind=kOutput, calls=%fused_computation.70 | convolution fusion | flops 268435456 | bytes 3276800 | tf_op jit(solution)/shard_map/dot_general | solution.py:264
  134.2 1.5 %fusion.1 = bf16[2048,256]{1,0:T(8,128)(2,1)} fusion(f32[2048,256]{1,0:T(8,128)S(1)} %fusion.18, f32[2048,256]{1,0:T(8,128)S(1)} %convolution_add_fusion.4, bf16[2048,256]{1,0:T(8,128)(2,1)S(1)} %bitcast.222, bf16[3,256,256]{2,1,0:T(8,128)(2,1)S(1)} %copy-done.5), kind=kOutput, calls=%fused_computation.17 | convolution fusion | flops 270008320 | bytes 6422528 | tf_op jit(solution)/shard_map/dot_general | solution.py:264
  (60 shorter events, 4.9 us)
Async XLA Ops:
  0.6 5.4 %copy-start.2 = (bf16[1,2,64,64,128]{4,3,2,1,0:T(8,128)(2,1)S(1)}, bf16[1,2,64,64,128]{4,3,2,1,0:T(8,128)(2,1)}, u32[]{:S(2)}) copy-start(bf16[1,2,64,64,128]{4,3,2,1,0:T(8,128)(2,1)} %param.6) | copy-start | bytes 6291460
  2.1 25.1 %collective-permute-start = (bf16[32,32,256]{2,1,0:T(8,128)(2,1)S(1)}, bf16[32,32,256]{2,1,0:T(8,128)(2,1)}, u32[]{:S(2)}, u32[]{:S(2)}) collective-permute-start(bf16[32,32,256]{2,1,0:T(8,128)(2,1)S(1)} %get-tuple-element.28), channel_id=1, source_target_pairs={{4,0},{5,1},{6,2},{7,3},{8,4},{9,5},{10,6},{11,7},{12,8},{13,9},{1... | collective-permute-start | bytes 1572872 | tf_op jit(solution)/shard_map/ppermute | solution.py:73
  3.4 30.2 %collective-permute-start.3 = (bf16[32,32,256]{2,1,0:T(8,128)(2,1)S(1)}, bf16[32,32,256]{2,1,0:T(8,128)(2,1)}, u32[]{:S(2)}, u32[]{:S(2)}) collective-permute-start(bf16[32,32,256]{2,1,0:T(8,128)(2,1)S(1)} %get-tuple-element.29), channel_id=1, source_target_pairs={{4,0},{5,1},{6,2},{7,3},{8,4},{9,5},{10,6},{11,7},{12,8},{13,9},{1... | collective-permute-start | bytes 1572872 | tf_op jit(solution)/shard_map/ppermute | solution.py:73
  4.7 50.2 %collective-permute-start.2 = (bf16[2,32,32,256]{3,2,1,0:T(8,128)(2,1)}, bf16[2,32,32,256]{3,2,1,0:T(8,128)(2,1)}, u32[]{:S(2)}, u32[]{:S(2)}) collective-permute-start(bf16[2,32,32,256]{3,2,1,0:T(8,128)(2,1)} %bitcast.19), channel_id=1, source_target_pairs={{2,0},{3,1},{6,4},{7,5},{10,8},{11,9},{14,12},{15,13},{18,16},{19,... | collective-permute-start | bytes 3145736 | tf_op jit(solution)/shard_map/ppermute | solution.py:213
  6.0 11.5 %copy-start.9 = (s32[256]{0:T(256)}, s32[256]{0:T(256)S(1)}, u32[]{:S(2)}) copy-start(s32[256]{0:T(256)S(1)} %get-tuple-element.31) | copy-start | bytes 3076
  6.0 11.5 %copy-start.11 = (s32[256]{0:T(256)}, s32[256]{0:T(256)S(1)}, u32[]{:S(2)}) copy-start(s32[256]{0:T(256)S(1)} %get-tuple-element.32) | copy-start | bytes 3076
  6.0 11.5 %copy-start.13 = (pred[256]{0:T(512)(128)(4,1)}, pred[256]{0:T(512)(128)(4,1)S(1)}, u32[]{:S(2)}) copy-start(pred[256]{0:T(512)(128)(4,1)S(1)} %compare_and_fusion) | copy-start | bytes 772
  10.5 1.1 copy-start.6
  10.7 1.3 copy-start.3
  12.9 0.9 copy-start
  16.2 2.1 %copy-start.7 = (f32[256]{0:T(256)S(1)}, f32[256]{0:T(256)}, u32[]{:S(2)}) copy-start(f32[256]{0:T(256)} %param.9) | copy-start | bytes 3076
  16.2 2.1 %copy-start.8 = (f32[256]{0:T(256)S(1)}, f32[256]{0:T(256)}, u32[]{:S(2)}) copy-start(f32[256]{0:T(256)} %param.8) | copy-start | bytes 3076
  17.1 18.5 %copy-start.5 = (bf16[3,256,256]{2,1,0:T(8,128)(2,1)S(1)}, bf16[3,256,256]{2,1,0:T(8,128)(2,1)}, u32[]{:S(2)}) copy-start(bf16[3,256,256]{2,1,0:T(8,128)(2,1)} %param.10) | copy-start | bytes 1179652
  17.5 0.6 copy-start.15
  20.0 36.3 %collective-permute-start.5 = (bf16[2,32,32,256]{3,2,1,0:T(8,128)(2,1)}, bf16[2,32,32,256]{3,2,1,0:T(8,128)(2,1)}, u32[]{:S(2)}, u32[]{:S(2)}) collective-permute-start(bf16[2,32,32,256]{3,2,1,0:T(8,128)(2,1)} %multiply_convert_fusion), channel_id=1, source_target_pairs={{0,4},{1,5},{2,6},{3,7},{4,8},{5,9},{6,10},{7,11},{8,12},{9,13},{1... | collective-permute-start | bytes 3145736 | tf_op jit(solution)/shard_map/ppermute | solution.py:73
  27.2 18.2 %collective-permute-start.1 = (bf16[32,32,256]{2,1,0:T(8,128)(2,1)}, bf16[32,32,256]{2,1,0:T(8,128)(2,1)}, u32[]{:S(2)}, u32[]{:S(2)}) collective-permute-start(bf16[32,32,256]{2,1,0:T(8,128)(2,1)} %collective-permute-done), channel_id=1, source_target_pairs={{0,2},{1,3},{4,6},{5,7},{8,10},{9,11},{12,14},{13,15},{16,18},{17,... | collective-permute-start | bytes 1572872 | tf_op jit(solution)/shard_map/ppermute | solution.py:214
  33.5 21.3 %collective-permute-start.4 = (bf16[32,32,256]{2,1,0:T(8,128)(2,1)}, bf16[32,32,256]{2,1,0:T(8,128)(2,1)}, u32[]{:S(2)}, u32[]{:S(2)}) collective-permute-start(bf16[32,32,256]{2,1,0:T(8,128)(2,1)} %collective-permute-done.3), channel_id=1, source_target_pairs={{0,2},{1,3},{4,6},{5,7},{8,10},{9,11},{12,14},{13,15},{16,18},{17,... | collective-permute-start | bytes 1572872 | tf_op jit(solution)/shard_map/ppermute | solution.py:214
  64.3 1.8 %copy-start.10 = (s32[256]{0:T(256)S(1)}, s32[256]{0:T(256)}, u32[]{:S(2)}) copy-start(s32[256]{0:T(256)} %copy-done.9) | copy-start | bytes 3076
  64.3 1.8 %copy-start.12 = (s32[256]{0:T(256)S(1)}, s32[256]{0:T(256)}, u32[]{:S(2)}) copy-start(s32[256]{0:T(256)} %copy-done.11) | copy-start | bytes 3076
  64.3 1.8 %copy-start.14 = (pred[256]{0:T(512)(128)(4,1)S(1)}, pred[256]{0:T(512)(128)(4,1)}, u32[]{:S(2)}) copy-start(pred[256]{0:T(512)(128)(4,1)} %copy-done.13) | copy-start | bytes 772
  64.3 1.8 %copy-start.16 = (f32[2,32]{1,0:T(2,128)S(1)}, f32[2,32]{1,0:T(2,128)}, u32[]{:S(2)}) copy-start(f32[2,32]{1,0:T(2,128)} %copy-done.15) | copy-start | bytes 772
  68.8 2.0 %copy-start.1 = (bf16[2,32,1,32,1,128]{5,3,4,2,1,0:T(8,128)(2,1)S(1)}, bf16[2,32,1,32,1,128]{5,3,4,2,1,0:T(8,128)(2,1)}, u32[]{:S(2)}) copy-start(bf16[2,32,1,32,1,128]{5,3,4,2,1,0:T(8,128)(2,1)} %copy-done) | copy-start | bytes 1572868
  71.1 1.1 copy-start.4
  75.3 58.8 %collective-permute-start.6 = (bf16[2,32,32,256]{3,2,1,0:T(8,128)(2,1)S(1)}, bf16[2,32,32,256]{3,2,1,0:T(8,128)(2,1)S(1)}, u32[]{:S(2)}, u32[]{:S(2)}) collective-permute-start(bf16[2,32,32,256]{3,2,1,0:T(8,128)(2,1)S(1)} %broadcast_select_fusion), channel_id=1, source_target_pairs={{0,2},{1,3},{2,0},{3,1},{4,6},{5,7},{6,4},{7,5},{8,10},{9,11},{10,... | collective-permute-start | bytes 3145736 | tf_op jit(solution)/shard_map/ppermute | solution.py:256

commit v3 on v2

--- a/solution.py
+++ b/solution.py
@@ -73,32 +73,43 @@
     return lax.ppermute(values, "tm", pairs)
 
 
-def bit_steps(clip_size, tm_size):
-    steps = [("clip", 1)] if clip_size > 1 else []
-    steps += [("tm", 1 << k) for k in range(tm_size.bit_length() - 1)]
-    steps += [("clip", 1 << k) for k in range(1, clip_size.bit_length() - 1)]
-    return steps
+def index_groups(clip_size, tm_size):
+    clip_bits = [1 << k for k in range(clip_size.bit_length() - 1)]
+    tm_bits = [1 << k for k in range(tm_size.bit_length() - 1)]
+    groups = [("clip", clip_bits[:1])] if clip_bits else []
+    groups += [("tm", tm_bits[k : k + 2]) for k in range(0, len(tm_bits), 2)]
+    groups += [("clip", clip_bits[k : k + 2]) for k in range(1, len(clip_bits), 2)]
+    return groups
 
 
 STREAMS = 2
 
 
-def sum_kernel(steps, sizes, *refs):
+def sum_kernel(groups, sizes, *refs):
     parts, refs = refs[: len(sizes)], refs[len(sizes) :]
     out_ref, acc, outgoing, incoming, rs_send, rs_recv, ag_send, ag_recv = refs
     place = {"clip": lax.axis_index("clip"), "tm": lax.axis_index("tm")}
-    bits, partners = [], []
-    for axis, weight in steps:
-        bit = (place[axis] // weight) % 2
-        other = place[axis] + weight * (1 - 2 * bit)
-        bits.append(bit)
-        partners.append((other, place["tm"]) if axis == "clip" else (place["clip"], other))
+    digits, peers = [], []
+    for axis, weights in groups:
+        bits = [(place[axis] // weight) % 2 for weight in weights]
+        digits.append(sum(bit * (1 << k) for k, bit in enumerate(bits)))
+        members = []
+        for flip in range(1, 1 << len(weights)):
+            other, digit = place[axis], 0
+            for k, weight in enumerate(weights):
+                flipped = (flip >> k) & 1
+                other = other + flipped * weight * (1 - 2 * bits[k])
+                digit = digit + (1 << k) * (1 - bits[k] if flipped else bits[k])
+            device = (other, place["tm"]) if axis == "clip" else (place["clip"], other)
+            members.append((device, digit))
+        peers.append(members)
 
     barrier = pltpu.get_barrier_semaphore()
-    for partner in partners:
-        pl.semaphore_signal(
-            barrier, inc=1, device_id=partner, device_id_type=pl.DeviceIdType.MESH
-        )
+    for members in peers:
+        for device, _ in members:
+            pl.semaphore_signal(
+                barrier, inc=1, device_id=device, device_id_type=pl.DeviceIdType.MESH
+            )
 
     _, devices, unit, chans = acc.shape
     flat = acc.reshape(STREAMS * devices * unit, chans)
@@ -107,74 +118,93 @@
         flat[row : row + size] = part[...].reshape(size, chans)
         row += size
     flat[row:] = jnp.zeros((flat.shape[0] - row, chans), jnp.float32)
-    pl.semaphore_wait(barrier, len(partners))
-
-    count = len(steps)
+    pl.semaphore_wait(barrier, sum(len(members) for members in peers))
+
+    count = len(groups)
     orders = [list(range(count)) for _ in range(STREAMS)]
     if count > 2:
         orders[1][1], orders[1][2] = 2, 1
+    pieces, slots = [], []
+    for order in orders:
+        size, slot = devices, 0
+        pieces.append([])
+        slots.append([])
+        for which in order:
+            size //= len(peers[which]) + 1
+            pieces[-1].append(size)
+            slots[-1].append(slot)
+            slot += size * len(peers[which])
     base = [0] * STREAMS
     kept = [[] for _ in range(STREAMS)]
-    flying = [None] * STREAMS
+    flying = [[] for _ in range(STREAMS)]
     copies = []
 
-    def send_half(stream, turn):
+    def send(stream, turn, index, source, target, sems):
         which = orders[stream][turn]
-        half = devices >> (turn + 1)
-        slot = pl.ds(devices - 2 * half, half)
-        give = base[stream] + (1 - bits[which]) * half
-        outgoing[stream, slot] = acc[stream, pl.ds(give, half)].astype(jnp.bfloat16)
+        sem = sum(len(members) for members in peers[:which]) + index
         copy = pltpu.make_async_remote_copy(
-            src_ref=outgoing.at[stream, slot],
-            dst_ref=incoming.at[stream, slot],
-            send_sem=rs_send.at[stream, turn],
-            recv_sem=rs_recv.at[stream, turn],
-            device_id=partners[which],
+            src_ref=source,
+            dst_ref=target,
+            send_sem=sems[0].at[stream, sem],
+            recv_sem=sems[1].at[stream, sem],
+            device_id=peers[which][index][0],
             device_id_type=pl.DeviceIdType.MESH,
         )
         copy.start()
         copies.append(copy)
-        flying[stream] = copy
-
-    def add_half(stream, turn):
+        flying[stream].append(copy)
+
+    def send_pieces(stream, turn):
+        size = pieces[stream][turn]
+        flying[stream] = []
+        for index, (_, digit) in enumerate(peers[orders[stream][turn]]):
+            slot = pl.ds(slots[stream][turn] + index * size, size)
+            give = pl.ds(base[stream] + digit * size, size)
+            outgoing[stream, slot] = acc[stream, give].astype(jnp.bfloat16)
+            send(
+                stream,
+                turn,
+                index,
+                outgoing.at[stream, slot],
+                incoming.at[stream, slot],
+                (rs_send, rs_recv),
+            )
+
+    def add_pieces(stream, turn):
         which = orders[stream][turn]
-        half = devices >> (turn + 1)
-        slot = pl.ds(devices - 2 * half, half)
-        keep = base[stream] + bits[which] * half
-        flying[stream].wait_recv()
-        acc[stream, pl.ds(keep, half)] += incoming[stream, slot].astype(jnp.float32)
-        kept[stream].append(keep)
-        base[stream] = keep
+        size = pieces[stream][turn]
+        base[stream] = base[stream] + digits[which] * size
+        keep = pl.ds(base[stream], size)
+        for copy in flying[stream]:
+            copy.wait_recv()
+        total = acc[stream, keep]
+        for index in range(len(peers[which])):
+            slot = pl.ds(slots[stream][turn] + index * size, size)
+            total = total + incoming[stream, slot].astype(jnp.float32)
+        acc[stream, keep] = total
+        kept[stream].append(base[stream])
 
     def send_held(stream, turn):
-        which = orders[stream][turn]
-        held = out_ref.at[stream, pl.ds(kept[stream][turn], devices >> (turn + 1))]
-        copy = pltpu.make_async_remote_copy(
-            src_ref=held,
-            dst_ref=held,
-            send_sem=ag_send.at[stream, turn],
-            recv_sem=ag_recv.at[stream, turn],
-            device_id=partners[which],
-            device_id_type=pl.DeviceIdType.MESH,
-        )
-        copy.start()
-        copies.append(copy)
-        flying[stream] = copy
+        held = out_ref.at[stream, pl.ds(kept[stream][turn], pieces[stream][turn])]
+        flying[stream] = []
+        for index in range(len(peers[orders[stream][turn]])):
+            send(stream, turn, index, held, held, (ag_send, ag_recv))
 
     for stream in range(STREAMS):
-        send_half(stream, 0)
+        send_pieces(stream, 0)
     for turn in range(count):
         for stream in range(STREAMS):
-            add_half(stream, turn)
+            add_pieces(stream, turn)
             if turn + 1 < count:
-                send_half(stream, turn + 1)
+                send_pieces(stream, turn + 1)
             else:
                 own = pl.ds(base[stream], 1)
                 out_ref[stream, own] = acc[stream, own].astype(jnp.bfloat16)
                 send_held(stream, turn)
     for turn in reversed(range(count)):
         for stream in range(STREAMS):
-            flying[stream].wait_recv()
+            for copy in flying[stream]:
+                copy.wait_recv()
             if turn > 0:
                 send_held(stream, turn - 1)
     for copy in copies:
@@ -183,13 +213,14 @@
 
 def sum_everywhere(parts, clip_size, tm_size):
     devices = clip_size * tm_size
-    steps = bit_steps(clip_size, tm_size)
+    groups = index_groups(clip_size, tm_size)
+    exchanges = sum((1 << len(weights)) - 1 for _, weights in groups)
     chans = parts[0].shape[-1]
     sizes = tuple(part.shape[0] for part in parts)
     unit = -(-sum(sizes) // (STREAMS * devices * 8)) * 8
     shape = (STREAMS, devices, unit, chans)
     total = pl.pallas_call(
-        functools.partial(sum_kernel, steps, sizes),
+        functools.partial(sum_kernel, groups, sizes),
         out_shape=jax.ShapeDtypeStruct(shape, jnp.bfloat16),
         in_specs=[pl.BlockSpec(memory_space=pltpu.VMEM)] * len(parts),
         out_specs=pl.BlockSpec(memory_space=pltpu.VMEM),
@@ -198,7 +229,7 @@
             pltpu.VMEM(shape, jnp.bfloat16),
             pltpu.VMEM(shape, jnp.bfloat16),
         ]
-        + [pltpu.SemaphoreType.DMA((STREAMS, len(steps)))] * 4,
+        + [pltpu.SemaphoreType.DMA((STREAMS, exchanges))] * 4,
         compiler_params=pltpu.CompilerParams(
             collective_id=0, has_side_effects=True, vmem_limit_bytes=32 * 1024 * 1024
         ),

time: 136 us -> 127 us (0.934)
  Pallas kernels: 50.3 us -> 40.9 us
    pallas_call x1, Pallas kernels: 50.3 us -> 40.9 us  [sum_everywhere(): pl.pallas_call(functools.partial(sum_kernel, groups, sizes), out_shape=ja...]
  transfers between devices with their start and end apart: 7 -> 7, of which waited for: 2 -> 2; matrix products, arithmetic and copies ran while one was open for 16% -> 17% of each run, Pallas kernels for 37% -> 32%
where the time goes in v3:
time: 127 us; the launch traced here: 126 us
  Pallas kernels  40.9 us (32%)
  matrix products  24.3 us (19%)
  starting transfers between devices  23.6 us (19%)
  waiting for transfers between devices  16 us (13%)
  local copies, waits for them, and re-layouts  11.6 us (9%)
  other arithmetic  8.84 us (7%)
    pallas_call x1, Pallas kernels, sum_everywhere(): pl.pallas_call(functools.partial(sum_kernel, groups, sizes), out_shape=ja...  40.9 us
    ppermute x2, waiting for transfers between devices, later_frames(): lax.ppermute(block, 'tm', [(low, low + hop) for low in lows])  16 us
    ppermute x3, starting transfers between devices, from_device(): return lax.ppermute(values, 'tm', pairs)  9.76 us
    ppermute x2, starting transfers between devices, later_frames(): lax.ppermute(block, 'tm', [(low, low + hop) for low in lows])  8.42 us
    dot_general x3, matrix products, per_device(): lax.dot_general(flat_acts, later, (((0,), (0,)), ((), ())), preferred_ele...  5.4 us
    dot_general x3, matrix products, per_device(): jnp.dot(earlier, temporal_weight[tap], preferred_element_type=jnp.float32)  5.14 us
    slice x1, local copies, waits for them, and re-layouts, split_phases(): viewed[:, :, row_phase, :, col_phase, :].reshape(-1, chans)  4.45 us
    dot_general x3, matrix products, per_device(): jnp.dot(later, temporal_weight[tap].T, preferred_element_type=jnp.float32)  4.29 us
  transfers between devices with their start and end apart: 7, of which 2 were waited for; matrix products, arithmetic and copies ran while one was open for 17% of the time, Pallas kernels for 32%

profile of v3, /device:TPU:0, one launch (start us, length us, event | category | flops | bytes accessed | tf_op | source)
XLA Modules:
  0.0 126.3 jit_solution(16605927495318988052)
XLA Ops:
  0.6 1.4 %slice_bitcast_fusion.3 = (bf16[32,32,256]{2,1,0:T(8,128)(2,1)S(1)}, bf16[32,32,256]{2,1,0:T(8,128)(2,1)S(1)}) fusion(bf16[1,2,32,32,256]{4,3,2,1,0:T(8,128)(2,1)} %param.11), kind=kLoop, calls=%fused_computation.67 | loop fusion | bytes 2097152 | tf_op jit(solution)/shard_map/unstack | solution.py:243
  2.1 1.3 %collective-permute-start = (bf16[32,32,256]{2,1,0:T(8,128)(2,1)S(1)}, bf16[32,32,256]{2,1,0:T(8,128)(2,1)}, u32[]{:S(2)}, u32[]{:S(2)}) collective-permute-start(bf16[32,32,256]{2,1,0:T(8,128)(2,1)S(1)} %get-tuple-element.28), channel_id=1, source_target_pairs={{4,0},{5,1},{6,2},{7,3},{8,4},{9,5},{10,6},{11,7},{12,8},{13,9},{1... | collective-permute-start | bytes 1572872 | tf_op jit(solution)/shard_map/ppermute | solution.py:73
  3.4 1.3 %collective-permute-start.3 = (bf16[32,32,256]{2,1,0:T(8,128)(2,1)S(1)}, bf16[32,32,256]{2,1,0:T(8,128)(2,1)}, u32[]{:S(2)}, u32[]{:S(2)}) collective-permute-start(bf16[32,32,256]{2,1,0:T(8,128)(2,1)S(1)} %get-tuple-element.29), channel_id=1, source_target_pairs={{4,0},{5,1},{6,2},{7,3},{8,4},{9,5},{10,6},{11,7},{12,8},{13,9},{1... | collective-permute-start | bytes 1572872 | tf_op jit(solution)/shard_map/ppermute | solution.py:73
  4.7 1.3 %collective-permute-start.2 = (bf16[2,32,32,256]{3,2,1,0:T(8,128)(2,1)}, bf16[2,32,32,256]{3,2,1,0:T(8,128)(2,1)}, u32[]{:S(2)}, u32[]{:S(2)}) collective-permute-start(bf16[2,32,32,256]{3,2,1,0:T(8,128)(2,1)} %bitcast.19), channel_id=1, source_target_pairs={{2,0},{3,1},{6,4},{7,5},{10,8},{11,9},{14,12},{15,13},{18,16},{19,... | collective-permute-start | bytes 3145736 | tf_op jit(solution)/shard_map/ppermute | solution.py:244
  6.0 4.5 %fusion.86 = (bf16[2,32,1,32,1,128]{5,4,3,2,1,0:T(2,128)(2,1)S(1)}, bf16[2,32,1,32,1,128]{5,4,3,2,1,0:T(2,128)(2,1)S(1)}, bf16[2,32,1,32,1,128]{5,4,3,2,1,0:T(2,128)(2,1)S(1)}, bf16[2,32,1,32,1,128]{5,4,3,2,1,0:T(2,128)(2,1)S(1)}) fusion(bf16[2,32,2,32,2,128]{5,4,3,2,1,0:T(2,128)(2,1)S(1)} %bitcast.215), kind=kLoop, calls=%fused_computation.145 | loop fusion | bytes 4194304 | tf_op jit(solution)/shard_map/slice | solution.py:39
  10.7 0.8 copy-done.6
  11.6 0.4 fusion.44
  12.0 0.4 fusion.36
  12.4 0.4 convolution_add_fusion.9
  12.9 0.4 fusion.39
  13.3 0.4 convolution_add_fusion.8
  13.9 0.4 fusion.14
  14.3 0.4 convolution_add_fusion.5
  14.7 0.4 convolution_add_fusion.6
  15.1 0.5 pad_slice_fusion
  15.6 0.6 fusion.83
  17.5 0.6 copy-done.15
  18.3 1.7 %multiply_convert_fusion = bf16[2,32,32,256]{3,2,1,0:T(8,128)(2,1)} fusion(f32[2,32,32,256]{3,2,1,0:T(8,128)S(1)} %get-tuple-element.17, f32[256]{0:T(256)S(1)} %copy-done.7, f32[256]{0:T(256)S(1)} %copy-done.8, f32[2,256]{1,0:T(2,128)S(1)} %fusion.26, f32[2,256]{1,0:T(2,128)S(1)} %fusion.27), kind=kLoop, calls=%fused_computation.29 | loop fusion | flops 4718592 | bytes 3151872 | tf_op jit(solution)/shard_map/convert_element_type | solution.py:277
  20.0 7.2 %collective-permute-start.5 = (bf16[2,32,32,256]{3,2,1,0:T(8,128)(2,1)}, bf16[2,32,32,256]{3,2,1,0:T(8,128)(2,1)}, u32[]{:S(2)}, u32[]{:S(2)}) collective-permute-start(bf16[2,32,32,256]{3,2,1,0:T(8,128)(2,1)} %multiply_convert_fusion), channel_id=1, source_target_pairs={{0,4},{1,5},{2,6},{3,7},{4,8},{5,9},{6,10},{7,11},{8,12},{9,13},{1... | collective-permute-start | bytes 3145736 | tf_op jit(solution)/shard_map/ppermute | solution.py:73
  27.2 6.3 %collective-permute-start.1 = (bf16[32,32,256]{2,1,0:T(8,128)(2,1)}, bf16[32,32,256]{2,1,0:T(8,128)(2,1)}, u32[]{:S(2)}, u32[]{:S(2)}) collective-permute-start(bf16[32,32,256]{2,1,0:T(8,128)(2,1)} %collective-permute-done), channel_id=1, source_target_pairs={{0,2},{1,3},{4,6},{5,7},{8,10},{9,11},{12,14},{13,15},{16,18},{17,... | collective-permute-start | bytes 1572872 | tf_op jit(solution)/shard_map/ppermute | solution.py:245
  33.5 2.1 %collective-permute-start.4 = (bf16[32,32,256]{2,1,0:T(8,128)(2,1)}, bf16[32,32,256]{2,1,0:T(8,128)(2,1)}, u32[]{:S(2)}, u32[]{:S(2)}) collective-permute-start(bf16[32,32,256]{2,1,0:T(8,128)(2,1)} %collective-permute-done.3), channel_id=1, source_target_pairs={{0,2},{1,3},{4,6},{5,7},{8,10},{9,11},{12,14},{13,15},{16,18},{17,... | collective-permute-start | bytes 1572872 | tf_op jit(solution)/shard_map/ppermute | solution.py:245
  35.6 2.0 %convolution_add_fusion.4 = f32[2048,256]{1,0:T(8,128)S(1)} fusion(bf16[2048,256]{1,0:T(8,128)(2,1)} %bitcast.17, bf16[3,256,256]{2,1,0:T(8,128)(2,1)S(1)} %copy-done.5), kind=kOutput, calls=%fused_computation.7 | convolution fusion | flops 269484032 | bytes 4325376 | tf_op jit(solution)/shard_map/dot_general | solution.py:295
  37.6 1.3 %pad_maximum_fusion.1 = bf16[2,32,32,256]{3,2,1,0:T(8,128)(2,1)S(1)} fusion(bf16[1,32,32,256]{3,2,1,0:T(8,128)(2,1)} %bitcast.27, bf16[1,32,32,256]{3,2,1,0:T(8,128)(2,1)} %bitcast.26), kind=kLoop, calls=%fused_computation.55 | loop fusion | flops 524288 | bytes 2097152 | tf_op jit(solution)/shard_map/stack | solution.py:247
  38.9 6.5 %collective-permute-done.1 = bf16[32,32,256]{2,1,0:T(8,128)(2,1)} collective-permute-done((bf16[32,32,256]{2,1,0:T(8,128)(2,1)}, bf16[32,32,256]{2,1,0:T(8,128)(2,1)}, u32[]{:S(2)}, u32[]{:S(2)}) %collective-permute-start.1) | collective-permute-done | bytes 524320 | tf_op jit(solution)/shard_map/ppermute | solution.py:245
  45.4 9.4 %collective-permute-done.4 = bf16[32,32,256]{2,1,0:T(8,128)(2,1)} collective-permute-done((bf16[32,32,256]{2,1,0:T(8,128)(2,1)}, bf16[32,32,256]{2,1,0:T(8,128)(2,1)}, u32[]{:S(2)}, u32[]{:S(2)}) %collective-permute-start.4) | collective-permute-done | bytes 524320 | tf_op jit(solution)/shard_map/ppermute | solution.py:245
  54.8 1.3 %fusion.13 = (bf16[1,32,32,256]{3,2,1,0:T(8,128)(2,1)S(1)}, bf16[1,32,32,256]{3,2,1,0:T(8,128)(2,1)S(1)}) fusion(bf16[32,32,256]{2,1,0:T(8,128)(2,1)} %collective-permute-done.1, bf16[2,32,32,256]{3,2,1,0:T(8,128)(2,1)} %collective-permute-done.2, pred[]{:T(512)S(6)} %eq.25, bf16[32,32,256]{2,1,0:T(8,128)(2,1)} %collective-permute-done.4), kind=kLoop, calls=%fused_computation.63 | loop fusion | flops 524288 | bytes 3145729 | tf_op jit(solution)/shard_map/stack | solution.py:247
  56.3 1.7 %convolution_bitcast_fusion.refs_11_ = f32[256,256]{1,0:T(8,128)S(1)} fusion(bf16[2,32,32,256]{3,2,1,0:T(8,128)(2,1)} %multiply_convert_fusion, bf16[2,32,32,256]{3,2,1,0:T(8,128)(2,1)S(1)} %pad_maximum_fusion.1), kind=kOutput, calls=%fused_computation.34 | convolution fusion | flops 268435456 | bytes 2359296 | tf_op jit(solution)/shard_map/dot_general | solution.py:302
  58.0 1.7 %convolution_bitcast_fusion.1.refs_10_ = f32[256,256]{1,0:T(8,128)S(1)} fusion(bf16[2,32,32,256]{3,2,1,0:T(8,128)(2,1)} %multiply_convert_fusion, bf16[2,32,32,256]{3,2,1,0:T(8,128)(2,1)S(1)} %pad_maximum_fusion), kind=kOutput, calls=%fused_computation.35 | convolution fusion | flops 268435456 | bytes 2359296 | tf_op jit(solution)/shard_map/dot_general | solution.py:302
  59.7 2.0 %convolution_bitcast_fusion.2.refs_9_ = f32[256,256]{1,0:T(8,128)S(1)} fusion(bf16[2,32,32,256]{3,2,1,0:T(8,128)(2,1)} %multiply_convert_fusion, bf16[2,32,32,256]{3,2,1,0:T(8,128)(2,1)} %bitcast.19), kind=kOutput, calls=%fused_computation.36 | convolution fusion | flops 268435456 | bytes 2359296 | tf_op jit(solution)/shard_map/dot_general | solution.py:302
  61.7 2.1 %convolution_add_fusion.2 = f32[2048,256]{1,0:T(8,128)S(1)} fusion(bf16[2048,256]{1,0:T(8,128)(2,1)} %bitcast.34, bf16[2048,256]{1,0:T(8,128)(2,1)} %bitcast.68, bf16[3,256,256]{2,1,0:T(8,128)(2,1)S(1)} %copy-done.5), kind=kOutput, calls=%fused_computation.4 | convolution fusion | flops 269484032 | bytes 4325376 | tf_op jit(solution)/shard_map/dot_general | solution.py:298
  63.8 0.5 convolution_add_fusion.1
  64.3 1.8 %multiply_reduce_fusion = (f32[256]{0:T(256)S(1)}, f32[256]{0:T(256)S(1)}, f32[2,256]{1,0:T(2,128)S(1)}, bf16[2048,256]{1,0:T(8,128)(2,1)S(1)}) fusion(f32[2,32,32,256]{3,2,1,0:T(8,128)S(1)} %get-tuple-element.17, f32[2,256]{1,0:T(2,128)S(1)} %fusion.26, f32[2,256]{1,0:T(2,128)S(1)} %fusion.27, f32[256]{0:T(256)S(1)} %copy-done.7, f32[256]{0:T(256)S(1)} %copy-done.8, ...), kind=kOutput, calls=%fused_computation.26 | convolution fusion | flops 279968768 | bytes 6432768 | tf_op jit(solution)/shard_map/dot_general | solution.py:298
  66.7 1.5 %fusion.16 = f32[2,256]{1,0:T(2,128)S(1)} fusion(f32[2,256]{1,0:T(2,128)S(1)} %fusion.25, f32[2,32,32,256]{3,2,1,0:T(8,128)S(1)} %get-tuple-element.17, f32[2,256]{1,0:T(2,128)S(1)} %fusion.27, f32[2,256]{1,0:T(2,128)S(1)} %fusion.26, f32[256]{0:T(256)S(1)} %copy-done.8, f32[256]{0:T(256)S(1)} %copy-done.7, bf16[2048,256]{1,0:T(8,128)(2,1)S(1)} %get-tuple-element.30), kind=kLoop, calls=%fused_computation.68 | loop fusion | flops 10485248 | bytes 3155968 | tf_op jit(solution)/shard_map/transpose(jvp())/reduce_sum | solution.py:63
  68.8 1.6 %add_convert_fusion = bf16[2,32,32,256]{3,2,1,0:T(8,128)(2,1)S(1)} fusion(f32[2,256]{1,0:T(2,128)S(1)} %fusion.24, f32[2,256]{1,0:T(2,128)S(1)} %fusion.25, f32[2,32,32,256]{3,2,1,0:T(8,128)S(1)} %get-tuple-element.17, f32[2,256]{1,0:T(2,128)S(1)} %fusion.27, f32[2,256]{1,0:T(2,128)S(1)} %fusion.26, f32[256]{0:T(256)S(1)} %copy-done.8, f32[256]{0:T(256)S(1)} %copy-done.7, ...), kind=kLoop, calls=%fused_computation.27 | loop fusion | flops 11010048 | bytes 4204544 | tf_op jit(solution)/shard_map/convert_element_type | solution.py:309
  70.4 0.4 convolution_bitcast_fusion.3.refs_8_
  71.1 0.7 pad_slice_fusion.5
  71.8 0.4 convolution_bitcast_fusion.6.refs_5_
  72.2 0.4 convolution_bitcast_fusion.7.refs_4_
  72.6 0.4 convolution_bitcast_fusion.5.refs_6_
  73.3 0.4 convolution_bitcast_fusion.9.refs_2_
  74.5 0.8 broadcast_select_fusion
  75.3 4.1 %collective-permute-start.6 = (bf16[2,32,32,256]{3,2,1,0:T(8,128)(2,1)S(1)}, bf16[2,32,32,256]{3,2,1,0:T(8,128)(2,1)S(1)}, u32[]{:S(2)}, u32[]{:S(2)}) collective-permute-start(bf16[2,32,32,256]{3,2,1,0:T(8,128)(2,1)S(1)} %broadcast_select_fusion), channel_id=1, source_target_pairs={{0,2},{1,3},{2,0},{3,1},{4,6},{5,7},{6,4},{7,5},{8,10},{9,11},{10,... | collective-permute-start | bytes 3145736 | tf_op jit(solution)/shard_map/ppermute | solution.py:287
  79.4 40.9 %shard_map.101 = bf16[2,32,32,256]{3,2,1,0:T(8,128)(2,1)S(1)} custom-call(f32[128,256]{1,0:T(8,128)S(1)} %convolution_bitcast_fusion.11.refs_0_, f32[128,256]{1,0:T(8,128)S(1)} %convolution_bitcast_fusion.10.refs_1_, f32[128,256]{1,0:T(8,128)S(1)} %convolution_bitcast_fusion.9.refs_2_, f32[128,256]{1,0:T(8,128)S(1)} %convolution_bitcast_fusion.8.refs_3_, ...), custom_call_target="tpu_custom_call" | custom-call | tf_op jit(solution)/shard_map/pallas_call | solution.py:222
  120.5 1.1 slice.128
  121.6 0.9 slice.131
  122.5 0.6 fusion.85
  123.1 1.6 %fusion.18 = f32[2048,256]{1,0:T(8,128)S(1)} fusion(bf16[2048,256]{1,0:T(8,128)(2,1)} %bitcast.30, bf16[3,256,256]{2,1,0:T(8,128)(2,1)S(1)} %copy-done.5), kind=kOutput, calls=%fused_computation.70 | convolution fusion | flops 268435456 | bytes 3276800 | tf_op jit(solution)/shard_map/dot_general | solution.py:295
  124.8 1.5 %fusion.1 = bf16[2048,256]{1,0:T(8,128)(2,1)} fusion(f32[2048,256]{1,0:T(8,128)S(1)} %fusion.18, f32[2048,256]{1,0:T(8,128)S(1)} %convolution_add_fusion.4, bf16[2048,256]{1,0:T(8,128)(2,1)S(1)} %bitcast.222, bf16[3,256,256]{2,1,0:T(8,128)(2,1)S(1)} %copy-done.5), kind=kOutput, calls=%fused_computation.17 | convolution fusion | flops 270008320 | bytes 6422528 | tf_op jit(solution)/shard_map/dot_general | solution.py:295
  (60 shorter events, 4.9 us)
Async XLA Ops:
  0.6 5.4 %copy-start.2 = (bf16[1,2,64,64,128]{4,3,2,1,0:T(8,128)(2,1)S(1)}, bf16[1,2,64,64,128]{4,3,2,1,0:T(8,128)(2,1)}, u32[]{:S(2)}) copy-start(bf16[1,2,64,64,128]{4,3,2,1,0:T(8,128)(2,1)} %param.6) | copy-start | bytes 6291460
  2.1 25.1 %collective-permute-start = (bf16[32,32,256]{2,1,0:T(8,128)(2,1)S(1)}, bf16[32,32,256]{2,1,0:T(8,128)(2,1)}, u32[]{:S(2)}, u32[]{:S(2)}) collective-permute-start(bf16[32,32,256]{2,1,0:T(8,128)(2,1)S(1)} %get-tuple-element.28), channel_id=1, source_target_pairs={{4,0},{5,1},{6,2},{7,3},{8,4},{9,5},{10,6},{11,7},{12,8},{13,9},{1... | collective-permute-start | bytes 1572872 | tf_op jit(solution)/shard_map/ppermute | solution.py:73
  3.4 30.2 %collective-permute-start.3 = (bf16[32,32,256]{2,1,0:T(8,128)(2,1)S(1)}, bf16[32,32,256]{2,1,0:T(8,128)(2,1)}, u32[]{:S(2)}, u32[]{:S(2)}) collective-permute-start(bf16[32,32,256]{2,1,0:T(8,128)(2,1)S(1)} %get-tuple-element.29), channel_id=1, source_target_pairs={{4,0},{5,1},{6,2},{7,3},{8,4},{9,5},{10,6},{11,7},{12,8},{13,9},{1... | collective-permute-start | bytes 1572872 | tf_op jit(solution)/shard_map/ppermute | solution.py:73
  4.7 50.2 %collective-permute-start.2 = (bf16[2,32,32,256]{3,2,1,0:T(8,128)(2,1)}, bf16[2,32,32,256]{3,2,1,0:T(8,128)(2,1)}, u32[]{:S(2)}, u32[]{:S(2)}) collective-permute-start(bf16[2,32,32,256]{3,2,1,0:T(8,128)(2,1)} %bitcast.19), channel_id=1, source_target_pairs={{2,0},{3,1},{6,4},{7,5},{10,8},{11,9},{14,12},{15,13},{18,16},{19,... | collective-permute-start | bytes 3145736 | tf_op jit(solution)/shard_map/ppermute | solution.py:244
  6.0 11.5 %copy-start.9 = (s32[256]{0:T(256)}, s32[256]{0:T(256)S(1)}, u32[]{:S(2)}) copy-start(s32[256]{0:T(256)S(1)} %get-tuple-element.31) | copy-start | bytes 3076
  6.0 11.5 %copy-start.11 = (s32[256]{0:T(256)}, s32[256]{0:T(256)S(1)}, u32[]{:S(2)}) copy-start(s32[256]{0:T(256)S(1)} %get-tuple-element.32) | copy-start | bytes 3076
  6.0 11.5 %copy-start.13 = (pred[256]{0:T(512)(128)(4,1)}, pred[256]{0:T(512)(128)(4,1)S(1)}, u32[]{:S(2)}) copy-start(pred[256]{0:T(512)(128)(4,1)S(1)} %compare_and_fusion) | copy-start | bytes 772
  10.5 1.1 copy-start.6
  10.7 1.3 %copy-start.3 = (bf16[2,32,1,32,1,128]{5,3,4,2,1,0:T(8,128)(2,1)}, bf16[2,32,1,32,1,128]{5,3,4,2,1,0:T(8,128)(2,1)S(1)}, u32[]{:S(2)}) copy-start(bf16[2,32,1,32,1,128]{5,3,4,2,1,0:T(8,128)(2,1)S(1)} %copy.53) | copy-start | bytes 1572868
  12.9 0.9 copy-start
  16.2 2.1 %copy-start.7 = (f32[256]{0:T(256)S(1)}, f32[256]{0:T(256)}, u32[]{:S(2)}) copy-start(f32[256]{0:T(256)} %param.9) | copy-start | bytes 3076
  16.2 2.1 %copy-start.8 = (f32[256]{0:T(256)S(1)}, f32[256]{0:T(256)}, u32[]{:S(2)}) copy-start(f32[256]{0:T(256)} %param.8) | copy-start | bytes 3076
  17.1 18.5 %copy-start.5 = (bf16[3,256,256]{2,1,0:T(8,128)(2,1)S(1)}, bf16[3,256,256]{2,1,0:T(8,128)(2,1)}, u32[]{:S(2)}) copy-start(bf16[3,256,256]{2,1,0:T(8,128)(2,1)} %param.10) | copy-start | bytes 1179652
  17.5 0.6 copy-start.15
  20.0 36.3 %collective-permute-start.5 = (bf16[2,32,32,256]{3,2,1,0:T(8,128)(2,1)}, bf16[2,32,32,256]{3,2,1,0:T(8,128)(2,1)}, u32[]{:S(2)}, u32[]{:S(2)}) collective-permute-start(bf16[2,32,32,256]{3,2,1,0:T(8,128)(2,1)} %multiply_convert_fusion), channel_id=1, source_target_pairs={{0,4},{1,5},{2,6},{3,7},{4,8},{5,9},{6,10},{7,11},{8,12},{9,13},{1... | collective-permute-start | bytes 3145736 | tf_op jit(solution)/shard_map/ppermute | solution.py:73
  27.2 18.2 %collective-permute-start.1 = (bf16[32,32,256]{2,1,0:T(8,128)(2,1)}, bf16[32,32,256]{2,1,0:T(8,128)(2,1)}, u32[]{:S(2)}, u32[]{:S(2)}) collective-permute-start(bf16[32,32,256]{2,1,0:T(8,128)(2,1)} %collective-permute-done), channel_id=1, source_target_pairs={{0,2},{1,3},{4,6},{5,7},{8,10},{9,11},{12,14},{13,15},{16,18},{17,... | collective-permute-start | bytes 1572872 | tf_op jit(solution)/shard_map/ppermute | solution.py:245
  33.5 21.3 %collective-permute-start.4 = (bf16[32,32,256]{2,1,0:T(8,128)(2,1)}, bf16[32,32,256]{2,1,0:T(8,128)(2,1)}, u32[]{:S(2)}, u32[]{:S(2)}) collective-permute-start(bf16[32,32,256]{2,1,0:T(8,128)(2,1)} %collective-permute-done.3), channel_id=1, source_target_pairs={{0,2},{1,3},{4,6},{5,7},{8,10},{9,11},{12,14},{13,15},{16,18},{17,... | collective-permute-start | bytes 1572872 | tf_op jit(solution)/shard_map/ppermute | solution.py:245
  64.3 1.8 %copy-start.10 = (s32[256]{0:T(256)S(1)}, s32[256]{0:T(256)}, u32[]{:S(2)}) copy-start(s32[256]{0:T(256)} %copy-done.9) | copy-start | bytes 3076
  64.3 1.8 %copy-start.12 = (s32[256]{0:T(256)S(1)}, s32[256]{0:T(256)}, u32[]{:S(2)}) copy-start(s32[256]{0:T(256)} %copy-done.11) | copy-start | bytes 3076
  64.3 1.8 %copy-start.14 = (pred[256]{0:T(512)(128)(4,1)S(1)}, pred[256]{0:T(512)(128)(4,1)}, u32[]{:S(2)}) copy-start(pred[256]{0:T(512)(128)(4,1)} %copy-done.13) | copy-start | bytes 772
  64.3 1.8 %copy-start.16 = (f32[2,32]{1,0:T(2,128)S(1)}, f32[2,32]{1,0:T(2,128)}, u32[]{:S(2)}) copy-start(f32[2,32]{1,0:T(2,128)} %copy-done.15) | copy-start | bytes 772
  68.8 2.0 %copy-start.1 = (bf16[2,32,1,32,1,128]{5,3,4,2,1,0:T(8,128)(2,1)S(1)}, bf16[2,32,1,32,1,128]{5,3,4,2,1,0:T(8,128)(2,1)}, u32[]{:S(2)}) copy-start(bf16[2,32,1,32,1,128]{5,3,4,2,1,0:T(8,128)(2,1)} %copy-done) | copy-start | bytes 1572868
  71.1 1.1 copy-start.4
  75.3 49.5 %collective-permute-start.6 = (bf16[2,32,32,256]{3,2,1,0:T(8,128)(2,1)S(1)}, bf16[2,32,32,256]{3,2,1,0:T(8,128)(2,1)S(1)}, u32[]{:S(2)}, u32[]{:S(2)}) collective-permute-start(bf16[2,32,32,256]{3,2,1,0:T(8,128)(2,1)S(1)} %broadcast_select_fusion), channel_id=1, source_target_pairs={{0,2},{1,3},{2,0},{3,1},{4,6},{5,7},{6,4},{7,5},{8,10},{9,11},{10,... | collective-permute-start | bytes 3145736 | tf_op jit(solution)/shard_map/ppermute | solution.py:287

commit v4 on v3

--- a/solution.py
+++ b/solution.py
@@ -82,7 +82,7 @@
     return groups
 
 
-STREAMS = 2
+STREAMS = 4
 
 
 def sum_kernel(groups, sizes, *refs):
@@ -123,7 +123,8 @@
     count = len(groups)
     orders = [list(range(count)) for _ in range(STREAMS)]
     if count > 2:
-        orders[1][1], orders[1][2] = 2, 1
+        for order in orders[1::2]:
+            order[1], order[2] = 2, 1
     pieces, slots = [], []
     for order in orders:
         size, slot = devices, 0

time: 127 us -> 126 us (level)
  no operation moved by 1% of the time
where the time goes in v4:
time: 126 us; the launch traced here: 125 us
  Pallas kernels  40 us (32%)
  matrix products  24.3 us (19%)
  starting transfers between devices  23.6 us (19%)
  waiting for transfers between devices  16 us (13%)
  local copies, waits for them, and re-layouts  11.6 us (9%)
  other arithmetic  8.84 us (7%)
    pallas_call x1, Pallas kernels, sum_everywhere(): pl.pallas_call(functools.partial(sum_kernel, groups, sizes), out_shape=ja...  40 us
    ppermute x2, waiting for transfers between devices, later_frames(): lax.ppermute(block, 'tm', [(low, low + hop) for low in lows])  16 us
    ppermute x3, starting transfers between devices, from_device(): return lax.ppermute(values, 'tm', pairs)  9.76 us
    ppermute x2, starting transfers between devices, later_frames(): lax.ppermute(block, 'tm', [(low, low + hop) for low in lows])  8.42 us
    dot_general x3, matrix products, per_device(): lax.dot_general(flat_acts, later, (((0,), (0,)), ((), ())), preferred_ele...  5.4 us
    dot_general x3, matrix products, per_device(): jnp.dot(earlier, temporal_weight[tap], preferred_element_type=jnp.float32)  5.14 us
    slice x1, local copies, waits for them, and re-layouts, split_phases(): viewed[:, :, row_phase, :, col_phase, :].reshape(-1, chans)  4.45 us
    dot_general x3, matrix products, per_device(): jnp.dot(later, temporal_weight[tap].T, preferred_element_type=jnp.float32)  4.29 us
  transfers between devices with their start and end apart: 7, of which 2 were waited for; matrix products, arithmetic and copies ran while one was open for 17% of the time, Pallas kernels for 32%

profile of v4, /device:TPU:0, one launch (start us, length us, event | category | flops | bytes accessed | tf_op | source)
XLA Modules:
  0.0 125.5 jit_solution(12305890302721065)
XLA Ops:
  0.6 1.4 %slice_bitcast_fusion.3 = (bf16[32,32,256]{2,1,0:T(8,128)(2,1)S(1)}, bf16[32,32,256]{2,1,0:T(8,128)(2,1)S(1)}) fusion(bf16[1,2,32,32,256]{4,3,2,1,0:T(8,128)(2,1)} %param.11), kind=kLoop, calls=%fused_computation.67 | loop fusion | bytes 2097152 | tf_op jit(solution)/shard_map/unstack | solution.py:244
  2.1 1.3 %collective-permute-start = (bf16[32,32,256]{2,1,0:T(8,128)(2,1)S(1)}, bf16[32,32,256]{2,1,0:T(8,128)(2,1)}, u32[]{:S(2)}, u32[]{:S(2)}) collective-permute-start(bf16[32,32,256]{2,1,0:T(8,128)(2,1)S(1)} %get-tuple-element.28), channel_id=1, source_target_pairs={{4,0},{5,1},{6,2},{7,3},{8,4},{9,5},{10,6},{11,7},{12,8},{13,9},{1... | collective-permute-start | bytes 1572872 | tf_op jit(solution)/shard_map/ppermute | solution.py:73
  3.4 1.3 %collective-permute-start.3 = (bf16[32,32,256]{2,1,0:T(8,128)(2,1)S(1)}, bf16[32,32,256]{2,1,0:T(8,128)(2,1)}, u32[]{:S(2)}, u32[]{:S(2)}) collective-permute-start(bf16[32,32,256]{2,1,0:T(8,128)(2,1)S(1)} %get-tuple-element.29), channel_id=1, source_target_pairs={{4,0},{5,1},{6,2},{7,3},{8,4},{9,5},{10,6},{11,7},{12,8},{13,9},{1... | collective-permute-start | bytes 1572872 | tf_op jit(solution)/shard_map/ppermute | solution.py:73
  4.7 1.3 %collective-permute-start.2 = (bf16[2,32,32,256]{3,2,1,0:T(8,128)(2,1)}, bf16[2,32,32,256]{3,2,1,0:T(8,128)(2,1)}, u32[]{:S(2)}, u32[]{:S(2)}) collective-permute-start(bf16[2,32,32,256]{3,2,1,0:T(8,128)(2,1)} %bitcast.19), channel_id=1, source_target_pairs={{2,0},{3,1},{6,4},{7,5},{10,8},{11,9},{14,12},{15,13},{18,16},{19,... | collective-permute-start | bytes 3145736 | tf_op jit(solution)/shard_map/ppermute | solution.py:245
  6.0 4.5 %fusion.86 = (bf16[2,32,1,32,1,128]{5,4,3,2,1,0:T(2,128)(2,1)S(1)}, bf16[2,32,1,32,1,128]{5,4,3,2,1,0:T(2,128)(2,1)S(1)}, bf16[2,32,1,32,1,128]{5,4,3,2,1,0:T(2,128)(2,1)S(1)}, bf16[2,32,1,32,1,128]{5,4,3,2,1,0:T(2,128)(2,1)S(1)}) fusion(bf16[2,32,2,32,2,128]{5,4,3,2,1,0:T(2,128)(2,1)S(1)} %bitcast.215), kind=kLoop, calls=%fused_computation.145 | loop fusion | bytes 4194304 | tf_op jit(solution)/shard_map/slice | solution.py:39
  10.7 0.8 copy-done.6
  11.6 0.4 fusion.44
  12.0 0.4 fusion.36
  12.4 0.4 convolution_add_fusion.9
  12.9 0.4 fusion.39
  13.3 0.4 convolution_add_fusion.8
  13.9 0.4 fusion.14
  14.3 0.4 convolution_add_fusion.5
  14.7 0.4 convolution_add_fusion.6
  15.1 0.5 pad_slice_fusion
  15.6 0.6 fusion.83
  17.5 0.6 copy-done.15
  18.3 1.7 %multiply_convert_fusion = bf16[2,32,32,256]{3,2,1,0:T(8,128)(2,1)} fusion(f32[2,32,32,256]{3,2,1,0:T(8,128)S(1)} %get-tuple-element.17, f32[256]{0:T(256)S(1)} %copy-done.7, f32[256]{0:T(256)S(1)} %copy-done.8, f32[2,256]{1,0:T(2,128)S(1)} %fusion.26, f32[2,256]{1,0:T(2,128)S(1)} %fusion.27), kind=kLoop, calls=%fused_computation.29 | loop fusion | flops 4718592 | bytes 3151872 | tf_op jit(solution)/shard_map/convert_element_type | solution.py:278
  20.0 7.2 %collective-permute-start.5 = (bf16[2,32,32,256]{3,2,1,0:T(8,128)(2,1)}, bf16[2,32,32,256]{3,2,1,0:T(8,128)(2,1)}, u32[]{:S(2)}, u32[]{:S(2)}) collective-permute-start(bf16[2,32,32,256]{3,2,1,0:T(8,128)(2,1)} %multiply_convert_fusion), channel_id=1, source_target_pairs={{0,4},{1,5},{2,6},{3,7},{4,8},{5,9},{6,10},{7,11},{8,12},{9,13},{1... | collective-permute-start | bytes 3145736 | tf_op jit(solution)/shard_map/ppermute | solution.py:73
  27.2 6.3 %collective-permute-start.1 = (bf16[32,32,256]{2,1,0:T(8,128)(2,1)}, bf16[32,32,256]{2,1,0:T(8,128)(2,1)}, u32[]{:S(2)}, u32[]{:S(2)}) collective-permute-start(bf16[32,32,256]{2,1,0:T(8,128)(2,1)} %collective-permute-done), channel_id=1, source_target_pairs={{0,2},{1,3},{4,6},{5,7},{8,10},{9,11},{12,14},{13,15},{16,18},{17,... | collective-permute-start | bytes 1572872 | tf_op jit(solution)/shard_map/ppermute | solution.py:246
  33.5 2.1 %collective-permute-start.4 = (bf16[32,32,256]{2,1,0:T(8,128)(2,1)}, bf16[32,32,256]{2,1,0:T(8,128)(2,1)}, u32[]{:S(2)}, u32[]{:S(2)}) collective-permute-start(bf16[32,32,256]{2,1,0:T(8,128)(2,1)} %collective-permute-done.3), channel_id=1, source_target_pairs={{0,2},{1,3},{4,6},{5,7},{8,10},{9,11},{12,14},{13,15},{16,18},{17,... | collective-permute-start | bytes 1572872 | tf_op jit(solution)/shard_map/ppermute | solution.py:246
  35.6 2.0 %convolution_add_fusion.4 = f32[2048,256]{1,0:T(8,128)S(1)} fusion(bf16[2048,256]{1,0:T(8,128)(2,1)} %bitcast.17, bf16[3,256,256]{2,1,0:T(8,128)(2,1)S(1)} %copy-done.5), kind=kOutput, calls=%fused_computation.7 | convolution fusion | flops 269484032 | bytes 4325376 | tf_op jit(solution)/shard_map/dot_general | solution.py:296
  37.6 1.3 %pad_maximum_fusion.1 = bf16[2,32,32,256]{3,2,1,0:T(8,128)(2,1)S(1)} fusion(bf16[1,32,32,256]{3,2,1,0:T(8,128)(2,1)} %bitcast.27, bf16[1,32,32,256]{3,2,1,0:T(8,128)(2,1)} %bitcast.26), kind=kLoop, calls=%fused_computation.55 | loop fusion | flops 524288 | bytes 2097152 | tf_op jit(solution)/shard_map/stack | solution.py:248
  38.9 6.5 %collective-permute-done.1 = bf16[32,32,256]{2,1,0:T(8,128)(2,1)} collective-permute-done((bf16[32,32,256]{2,1,0:T(8,128)(2,1)}, bf16[32,32,256]{2,1,0:T(8,128)(2,1)}, u32[]{:S(2)}, u32[]{:S(2)}) %collective-permute-start.1) | collective-permute-done | bytes 524320 | tf_op jit(solution)/shard_map/ppermute | solution.py:246
  45.4 9.4 %collective-permute-done.4 = bf16[32,32,256]{2,1,0:T(8,128)(2,1)} collective-permute-done((bf16[32,32,256]{2,1,0:T(8,128)(2,1)}, bf16[32,32,256]{2,1,0:T(8,128)(2,1)}, u32[]{:S(2)}, u32[]{:S(2)}) %collective-permute-start.4) | collective-permute-done | bytes 524320 | tf_op jit(solution)/shard_map/ppermute | solution.py:246
  54.8 1.3 %fusion.13 = (bf16[1,32,32,256]{3,2,1,0:T(8,128)(2,1)S(1)}, bf16[1,32,32,256]{3,2,1,0:T(8,128)(2,1)S(1)}) fusion(bf16[32,32,256]{2,1,0:T(8,128)(2,1)} %collective-permute-done.1, bf16[2,32,32,256]{3,2,1,0:T(8,128)(2,1)} %collective-permute-done.2, pred[]{:T(512)S(6)} %eq.25, bf16[32,32,256]{2,1,0:T(8,128)(2,1)} %collective-permute-done.4), kind=kLoop, calls=%fused_computation.63 | loop fusion | flops 524288 | bytes 3145729 | tf_op jit(solution)/shard_map/stack | solution.py:248
  56.3 1.7 %convolution_bitcast_fusion.refs_11_ = f32[256,256]{1,0:T(8,128)S(1)} fusion(bf16[2,32,32,256]{3,2,1,0:T(8,128)(2,1)} %multiply_convert_fusion, bf16[2,32,32,256]{3,2,1,0:T(8,128)(2,1)S(1)} %pad_maximum_fusion.1), kind=kOutput, calls=%fused_computation.34 | convolution fusion | flops 268435456 | bytes 2359296 | tf_op jit(solution)/shard_map/dot_general | solution.py:303
  58.0 1.7 %convolution_bitcast_fusion.1.refs_10_ = f32[256,256]{1,0:T(8,128)S(1)} fusion(bf16[2,32,32,256]{3,2,1,0:T(8,128)(2,1)} %multiply_convert_fusion, bf16[2,32,32,256]{3,2,1,0:T(8,128)(2,1)S(1)} %pad_maximum_fusion), kind=kOutput, calls=%fused_computation.35 | convolution fusion | flops 268435456 | bytes 2359296 | tf_op jit(solution)/shard_map/dot_general | solution.py:303
  59.7 2.0 %convolution_bitcast_fusion.2.refs_9_ = f32[256,256]{1,0:T(8,128)S(1)} fusion(bf16[2,32,32,256]{3,2,1,0:T(8,128)(2,1)} %multiply_convert_fusion, bf16[2,32,32,256]{3,2,1,0:T(8,128)(2,1)} %bitcast.19), kind=kOutput, calls=%fused_computation.36 | convolution fusion | flops 268435456 | bytes 2359296 | tf_op jit(solution)/shard_map/dot_general | solution.py:303
  61.7 2.1 %convolution_add_fusion.2 = f32[2048,256]{1,0:T(8,128)S(1)} fusion(bf16[2048,256]{1,0:T(8,128)(2,1)} %bitcast.34, bf16[2048,256]{1,0:T(8,128)(2,1)} %bitcast.68, bf16[3,256,256]{2,1,0:T(8,128)(2,1)S(1)} %copy-done.5), kind=kOutput, calls=%fused_computation.4 | convolution fusion | flops 269484032 | bytes 4325376 | tf_op jit(solution)/shard_map/dot_general | solution.py:299
  63.8 0.5 convolution_add_fusion.1
  64.3 1.8 %multiply_reduce_fusion = (f32[256]{0:T(256)S(1)}, f32[256]{0:T(256)S(1)}, f32[2,256]{1,0:T(2,128)S(1)}, bf16[2048,256]{1,0:T(8,128)(2,1)S(1)}) fusion(f32[2,32,32,256]{3,2,1,0:T(8,128)S(1)} %get-tuple-element.17, f32[2,256]{1,0:T(2,128)S(1)} %fusion.26, f32[2,256]{1,0:T(2,128)S(1)} %fusion.27, f32[256]{0:T(256)S(1)} %copy-done.7, f32[256]{0:T(256)S(1)} %copy-done.8, ...), kind=kOutput, calls=%fused_computation.26 | convolution fusion | flops 279968768 | bytes 6432768 | tf_op jit(solution)/shard_map/dot_general | solution.py:299
  66.7 1.5 %fusion.16 = f32[2,256]{1,0:T(2,128)S(1)} fusion(f32[2,256]{1,0:T(2,128)S(1)} %fusion.25, f32[2,32,32,256]{3,2,1,0:T(8,128)S(1)} %get-tuple-element.17, f32[2,256]{1,0:T(2,128)S(1)} %fusion.27, f32[2,256]{1,0:T(2,128)S(1)} %fusion.26, f32[256]{0:T(256)S(1)} %copy-done.8, f32[256]{0:T(256)S(1)} %copy-done.7, bf16[2048,256]{1,0:T(8,128)(2,1)S(1)} %get-tuple-element.30), kind=kLoop, calls=%fused_computation.68 | loop fusion | flops 10485248 | bytes 3155968 | tf_op jit(solution)/shard_map/transpose(jvp())/reduce_sum | solution.py:63
  68.8 1.6 %add_convert_fusion = bf16[2,32,32,256]{3,2,1,0:T(8,128)(2,1)S(1)} fusion(f32[2,256]{1,0:T(2,128)S(1)} %fusion.24, f32[2,256]{1,0:T(2,128)S(1)} %fusion.25, f32[2,32,32,256]{3,2,1,0:T(8,128)S(1)} %get-tuple-element.17, f32[2,256]{1,0:T(2,128)S(1)} %fusion.27, f32[2,256]{1,0:T(2,128)S(1)} %fusion.26, f32[256]{0:T(256)S(1)} %copy-done.8, f32[256]{0:T(256)S(1)} %copy-done.7, ...), kind=kLoop, calls=%fused_computation.27 | loop fusion | flops 11010048 | bytes 4204544 | tf_op jit(solution)/shard_map/convert_element_type | solution.py:310
  70.4 0.4 convolution_bitcast_fusion.3.refs_8_
  71.1 0.7 pad_slice_fusion.5
  71.8 0.4 convolution_bitcast_fusion.6.refs_5_
  72.2 0.4 convolution_bitcast_fusion.7.refs_4_
  72.6 0.4 convolution_bitcast_fusion.5.refs_6_
  73.3 0.4 convolution_bitcast_fusion.9.refs_2_
  74.5 0.8 broadcast_select_fusion
  75.3 4.1 %collective-permute-start.6 = (bf16[2,32,32,256]{3,2,1,0:T(8,128)(2,1)S(1)}, bf16[2,32,32,256]{3,2,1,0:T(8,128)(2,1)S(1)}, u32[]{:S(2)}, u32[]{:S(2)}) collective-permute-start(bf16[2,32,32,256]{3,2,1,0:T(8,128)(2,1)S(1)} %broadcast_select_fusion), channel_id=1, source_target_pairs={{0,2},{1,3},{2,0},{3,1},{4,6},{5,7},{6,4},{7,5},{8,10},{9,11},{10,... | collective-permute-start | bytes 3145736 | tf_op jit(solution)/shard_map/ppermute | solution.py:288
  79.4 40.0 %shard_map.101 = bf16[4,32,16,256]{3,2,1,0:T(8,128)(2,1)S(1)} custom-call(f32[128,256]{1,0:T(8,128)S(1)} %convolution_bitcast_fusion.11.refs_0_, f32[128,256]{1,0:T(8,128)S(1)} %convolution_bitcast_fusion.10.refs_1_, f32[128,256]{1,0:T(8,128)S(1)} %convolution_bitcast_fusion.9.refs_2_, f32[128,256]{1,0:T(8,128)S(1)} %convolution_bitcast_fusion.8.refs_3_, ...), custom_call_target="tpu_custom_call" | custom-call | tf_op jit(solution)/shard_map/pallas_call | solution.py:223
  119.7 1.1 slice.128
  120.8 0.9 slice.131
  121.7 0.6 fusion.85
  122.3 1.7 %fusion.18 = f32[2048,256]{1,0:T(8,128)S(1)} fusion(bf16[2048,256]{1,0:T(8,128)(2,1)} %bitcast.30, bf16[3,256,256]{2,1,0:T(8,128)(2,1)S(1)} %copy-done.5), kind=kOutput, calls=%fused_computation.70 | convolution fusion | flops 268435456 | bytes 3276800 | tf_op jit(solution)/shard_map/dot_general | solution.py:296
  123.9 1.5 %fusion.1 = bf16[2048,256]{1,0:T(8,128)(2,1)} fusion(f32[2048,256]{1,0:T(8,128)S(1)} %fusion.18, f32[2048,256]{1,0:T(8,128)S(1)} %convolution_add_fusion.4, bf16[2048,256]{1,0:T(8,128)(2,1)S(1)} %bitcast.222, bf16[3,256,256]{2,1,0:T(8,128)(2,1)S(1)} %copy-done.5), kind=kOutput, calls=%fused_computation.17 | convolution fusion | flops 270008320 | bytes 6422528 | tf_op jit(solution)/shard_map/dot_general | solution.py:296
  (60 shorter events, 4.9 us)
Async XLA Ops:
  0.6 5.4 %copy-start.2 = (bf16[1,2,64,64,128]{4,3,2,1,0:T(8,128)(2,1)S(1)}, bf16[1,2,64,64,128]{4,3,2,1,0:T(8,128)(2,1)}, u32[]{:S(2)}) copy-start(bf16[1,2,64,64,128]{4,3,2,1,0:T(8,128)(2,1)} %param.6) | copy-start | bytes 6291460
  2.1 25.1 %collective-permute-start = (bf16[32,32,256]{2,1,0:T(8,128)(2,1)S(1)}, bf16[32,32,256]{2,1,0:T(8,128)(2,1)}, u32[]{:S(2)}, u32[]{:S(2)}) collective-permute-start(bf16[32,32,256]{2,1,0:T(8,128)(2,1)S(1)} %get-tuple-element.28), channel_id=1, source_target_pairs={{4,0},{5,1},{6,2},{7,3},{8,4},{9,5},{10,6},{11,7},{12,8},{13,9},{1... | collective-permute-start | bytes 1572872 | tf_op jit(solution)/shard_map/ppermute | solution.py:73
  3.4 30.2 %collective-permute-start.3 = (bf16[32,32,256]{2,1,0:T(8,128)(2,1)S(1)}, bf16[32,32,256]{2,1,0:T(8,128)(2,1)}, u32[]{:S(2)}, u32[]{:S(2)}) collective-permute-start(bf16[32,32,256]{2,1,0:T(8,128)(2,1)S(1)} %get-tuple-element.29), channel_id=1, source_target_pairs={{4,0},{5,1},{6,2},{7,3},{8,4},{9,5},{10,6},{11,7},{12,8},{13,9},{1... | collective-permute-start | bytes 1572872 | tf_op jit(solution)/shard_map/ppermute | solution.py:73
  4.7 50.2 %collective-permute-start.2 = (bf16[2,32,32,256]{3,2,1,0:T(8,128)(2,1)}, bf16[2,32,32,256]{3,2,1,0:T(8,128)(2,1)}, u32[]{:S(2)}, u32[]{:S(2)}) collective-permute-start(bf16[2,32,32,256]{3,2,1,0:T(8,128)(2,1)} %bitcast.19), channel_id=1, source_target_pairs={{2,0},{3,1},{6,4},{7,5},{10,8},{11,9},{14,12},{15,13},{18,16},{19,... | collective-permute-start | bytes 3145736 | tf_op jit(solution)/shard_map/ppermute | solution.py:245
  6.0 11.5 %copy-start.9 = (s32[256]{0:T(256)}, s32[256]{0:T(256)S(1)}, u32[]{:S(2)}) copy-start(s32[256]{0:T(256)S(1)} %get-tuple-element.31) | copy-start | bytes 3076
  6.0 11.5 %copy-start.11 = (s32[256]{0:T(256)}, s32[256]{0:T(256)S(1)}, u32[]{:S(2)}) copy-start(s32[256]{0:T(256)S(1)} %get-tuple-element.32) | copy-start | bytes 3076
  6.0 11.5 %copy-start.13 = (pred[256]{0:T(512)(128)(4,1)}, pred[256]{0:T(512)(128)(4,1)S(1)}, u32[]{:S(2)}) copy-start(pred[256]{0:T(512)(128)(4,1)S(1)} %compare_and_fusion) | copy-start | bytes 772
  10.5 1.1 copy-start.6
  10.7 1.3 %copy-start.3 = (bf16[2,32,1,32,1,128]{5,3,4,2,1,0:T(8,128)(2,1)}, bf16[2,32,1,32,1,128]{5,3,4,2,1,0:T(8,128)(2,1)S(1)}, u32[]{:S(2)}) copy-start(bf16[2,32,1,32,1,128]{5,3,4,2,1,0:T(8,128)(2,1)S(1)} %copy.53) | copy-start | bytes 1572868
  12.9 0.9 copy-start
  16.2 2.1 %copy-start.7 = (f32[256]{0:T(256)S(1)}, f32[256]{0:T(256)}, u32[]{:S(2)}) copy-start(f32[256]{0:T(256)} %param.9) | copy-start | bytes 3076
  16.2 2.1 %copy-start.8 = (f32[256]{0:T(256)S(1)}, f32[256]{0:T(256)}, u32[]{:S(2)}) copy-start(f32[256]{0:T(256)} %param.8) | copy-start | bytes 3076
  17.1 18.5 %copy-start.5 = (bf16[3,256,256]{2,1,0:T(8,128)(2,1)S(1)}, bf16[3,256,256]{2,1,0:T(8,128)(2,1)}, u32[]{:S(2)}) copy-start(bf16[3,256,256]{2,1,0:T(8,128)(2,1)} %param.10) | copy-start | bytes 1179652
  17.5 0.6 copy-start.15
  20.0 36.3 %collective-permute-start.5 = (bf16[2,32,32,256]{3,2,1,0:T(8,128)(2,1)}, bf16[2,32,32,256]{3,2,1,0:T(8,128)(2,1)}, u32[]{:S(2)}, u32[]{:S(2)}) collective-permute-start(bf16[2,32,32,256]{3,2,1,0:T(8,128)(2,1)} %multiply_convert_fusion), channel_id=1, source_target_pairs={{0,4},{1,5},{2,6},{3,7},{4,8},{5,9},{6,10},{7,11},{8,12},{9,13},{1... | collective-permute-start | bytes 3145736 | tf_op jit(solution)/shard_map/ppermute | solution.py:73
  27.2 18.2 %collective-permute-start.1 = (bf16[32,32,256]{2,1,0:T(8,128)(2,1)}, bf16[32,32,256]{2,1,0:T(8,128)(2,1)}, u32[]{:S(2)}, u32[]{:S(2)}) collective-permute-start(bf16[32,32,256]{2,1,0:T(8,128)(2,1)} %collective-permute-done), channel_id=1, source_target_pairs={{0,2},{1,3},{4,6},{5,7},{8,10},{9,11},{12,14},{13,15},{16,18},{17,... | collective-permute-start | bytes 1572872 | tf_op jit(solution)/shard_map/ppermute | solution.py:246
  33.5 21.3 %collective-permute-start.4 = (bf16[32,32,256]{2,1,0:T(8,128)(2,1)}, bf16[32,32,256]{2,1,0:T(8,128)(2,1)}, u32[]{:S(2)}, u32[]{:S(2)}) collective-permute-start(bf16[32,32,256]{2,1,0:T(8,128)(2,1)} %collective-permute-done.3), channel_id=1, source_target_pairs={{0,2},{1,3},{4,6},{5,7},{8,10},{9,11},{12,14},{13,15},{16,18},{17,... | collective-permute-start | bytes 1572872 | tf_op jit(solution)/shard_map/ppermute | solution.py:246
  64.3 1.8 %copy-start.10 = (s32[256]{0:T(256)S(1)}, s32[256]{0:T(256)}, u32[]{:S(2)}) copy-start(s32[256]{0:T(256)} %copy-done.9) | copy-start | bytes 3076
  64.3 1.8 %copy-start.12 = (s32[256]{0:T(256)S(1)}, s32[256]{0:T(256)}, u32[]{:S(2)}) copy-start(s32[256]{0:T(256)} %copy-done.11) | copy-start | bytes 3076
  64.3 1.8 %copy-start.14 = (pred[256]{0:T(512)(128)(4,1)S(1)}, pred[256]{0:T(512)(128)(4,1)}, u32[]{:S(2)}) copy-start(pred[256]{0:T(512)(128)(4,1)} %copy-done.13) | copy-start | bytes 772
  64.3 1.8 %copy-start.16 = (f32[2,32]{1,0:T(2,128)S(1)}, f32[2,32]{1,0:T(2,128)}, u32[]{:S(2)}) copy-start(f32[2,32]{1,0:T(2,128)} %copy-done.15) | copy-start | bytes 772
  68.8 2.0 %copy-start.1 = (bf16[2,32,1,32,1,128]{5,3,4,2,1,0:T(8,128)(2,1)S(1)}, bf16[2,32,1,32,1,128]{5,3,4,2,1,0:T(8,128)(2,1)}, u32[]{:S(2)}) copy-start(bf16[2,32,1,32,1,128]{5,3,4,2,1,0:T(8,128)(2,1)} %copy-done) | copy-start | bytes 1572868
  71.1 1.1 copy-start.4
  75.3 48.6 %collective-permute-start.6 = (bf16[2,32,32,256]{3,2,1,0:T(8,128)(2,1)S(1)}, bf16[2,32,32,256]{3,2,1,0:T(8,128)(2,1)S(1)}, u32[]{:S(2)}, u32[]{:S(2)}) collective-permute-start(bf16[2,32,32,256]{3,2,1,0:T(8,128)(2,1)S(1)} %broadcast_select_fusion), channel_id=1, source_target_pairs={{0,2},{1,3},{2,0},{3,1},{4,6},{5,7},{6,4},{7,5},{8,10},{9,11},{10,... | collective-permute-start | bytes 3145736 | tf_op jit(solution)/shard_map/ppermute | solution.py:288
